TPU v7x, 32 devices: a whole 2x2x4 slice. The times are simulated.
32 devices in a mesh: dp: 4 (over y, x), expert: 8 (over z, core).
Axes of the slice: x: 2, y: 2, z: 4, core: 2. Of those that a mesh axis runs over, the one named last changes fastest.
Arguments:
- tokens: bfloat16 [1024, 2048], P(('dp', 'expert')), may hold values from -6 to 6
- grad_out: bfloat16 [1024, 2048], P(('dp', 'expert')), may hold values from -0.59765625 to 0.59765625
- routing: int32 [1024, 8], P(('dp', 'expert')), may hold values from 0 to 15, as said below
- replica: int32 [1024, 8], P(('dp', 'expert')), may hold values from 0 to 1, as said below
- gates: bfloat16 [1024, 8], P(('dp', 'expert')), may hold values from 0.25 to 4
- host_expert: int32 [8], replicated, may hold values from 0 to 15, as said below
- w_gate_up: bfloat16 [16, 2, 768, 2048], P('expert', None, 'dp'), may hold values from -0.125 to 0.125
- w_down: bfloat16 [16, 768, 2048], P('expert', 'dp'), may hold values from -0.21875 to 0.21875
Outputs:
- grad_tokens: bfloat16 [1024, 2048], P(('dp', 'expert'))
- grad_gates: float32 [1024, 8], P(('dp', 'expert'))
- grad_w_gate_up: bfloat16 [16, 2, 768, 2048], P('expert', None, 'dp')
- grad_w_down: bfloat16 [16, 768, 2048], P('expert', 'dp')
Inputs may be any that keep to these rules, and one draw needn't show every extreme that they name: `routing`: column k of a token names an expert of 2 * k to 2 * k + 1. Within the rows of one device, experts 2 i and 2 i + 1 are named together exactly 2 * 16 times. `replica`: within the rows of one device, each expert has at most 16 choices marked 0 and at most 16 marked 1; some expert reaches 16 marked 0 from every device, and in every index of dp some expert reaches 16 marked 1 from every device. Only experts listed in host_expert have choices marked 1. `host_expert`: for every device d of the expert axis exactly one of its experts 2 d and 2 d + 1 is listed, and it is listed once.
All inputs are finite; a program needn't handle non-finite values.
Results may differ from a plain program's by a relative error of at most 0.013.
Values may be sent and summed in bfloat16 or wider, within the bound.
A program may use at most 128 MiB of HBM per device.

v0:
```python
import jax
import jax.numpy as jnp
from jax import lax
from jax.sharding import PartitionSpec as P


def lookup(values_table, indices):
    matches = indices[..., None] == lax.broadcasted_iota(
        jnp.int32, indices.shape + values_table.shape, indices.ndim
    )
    return jnp.sum(jnp.where(matches, values_table, 0), axis=-1)


def placement(host_expert, owned_experts, devices):
    experts = owned_experts * devices
    matches = host_expert[None, :] == lax.broadcasted_iota(jnp.int32, (experts, devices), 0)
    helper_ids = lax.broadcasted_iota(jnp.int32, (experts, devices), 1)
    helper_of = jnp.sum(jnp.where(matches, helper_ids, 0), axis=1)
    listed = jnp.sum(matches.astype(jnp.int32), axis=1)
    return (helper_of, listed)


def targets(routing, replica, host_expert, owned_experts, devices, slot_rows, groups):
    helper_of, listed = placement(host_expert, owned_experts, devices)
    choices = routing.shape[0] // groups * routing.shape[1]
    usable = (replica == 0) | (lookup(listed, routing) > 0)
    device_to = jnp.where(replica == 0, routing // owned_experts, lookup(helper_of, routing))
    block_to = jnp.where(replica == 0, routing % owned_experts, owned_experts)
    labels = (routing * 2 + replica).reshape(groups, choices)
    earlier = lax.broadcasted_iota(jnp.int32, (choices, choices), 1) < lax.broadcasted_iota(
        jnp.int32, (choices, choices), 0
    )
    matching = (labels[:, :, None] == labels[:, None, :]) & earlier[None]
    ranking = jnp.sum(matching.astype(jnp.int32), axis=2).reshape(routing.shape)
    group_ids = lax.broadcasted_iota(jnp.int32, (groups, choices), 0).reshape(routing.shape)
    position = ((block_to * groups + group_ids) * devices + device_to) * slot_rows + ranking
    return jnp.where(usable, position, -1)


def selector(position, total_slots):
    matches = position[None, :, :] == lax.broadcasted_iota(
        jnp.int32, (total_slots,) + position.shape, 0
    )
    picker = jnp.sum(matches.astype(jnp.float32), axis=2).astype(jnp.bfloat16)
    return (matches, picker)


def fill_rows(matches, picker, tokens, grad_out, gates):
    row_x = jnp.dot(picker, tokens, preferred_element_type=jnp.float32).astype(jnp.bfloat16)
    row_dy = jnp.dot(picker, grad_out, preferred_element_type=jnp.float32).astype(jnp.bfloat16)
    row_gate = jnp.sum(
        jnp.where(matches, gates[None].astype(jnp.float32), 0.0), axis=(1, 2)
    ).astype(jnp.bfloat16)
    return (row_x, row_dy, row_gate)


def expert_block(inputs, upstream, weight, gate_up, down_matrix):
    mixed = jnp.einsum("rd,jfd->jrf", inputs, gate_up, preferred_element_type=jnp.float32)
    gate_pre = mixed[0]
    up_part = mixed[1]
    sigmoid_gate = jax.nn.sigmoid(gate_pre)
    active = gate_pre * sigmoid_gate
    hidden = (active * up_part).astype(jnp.bfloat16)
    output_part = jnp.einsum("rf,fd->rd", hidden, down_matrix, preferred_element_type=jnp.float32)
    gate_part = jnp.sum(output_part * upstream.astype(jnp.float32), axis=1)
    scaled = (weight.astype(jnp.float32)[:, None] * upstream.astype(jnp.float32)).astype(
        jnp.bfloat16
    )
    grad_hidden = jnp.einsum("rd,fd->rf", scaled, down_matrix, preferred_element_type=jnp.float32)
    grad_gate = grad_hidden * up_part * sigmoid_gate * (1.0 + gate_pre * (1.0 - sigmoid_gate))
    grad_mixed = jnp.stack([grad_gate, grad_hidden * active], axis=0).astype(jnp.bfloat16)
    input_part = jnp.einsum("jrf,jfd->rd", grad_mixed, gate_up, preferred_element_type=jnp.float32)
    weight_gu = jnp.einsum("jrf,rd->jfd", grad_mixed, inputs, preferred_element_type=jnp.float32)
    weight_down = jnp.einsum("rf,rd->fd", hidden, scaled, preferred_element_type=jnp.float32)
    return (input_part, gate_part, weight_gu, weight_down)


def shards(tokens, grad_out, routing, replica, gates, host_expert, w_gate_up, w_down):
    devices = lax.axis_size("expert")
    device_id = lax.axis_index("expert")
    token_rows, features = tokens.shape
    owned_experts = w_gate_up.shape[0]
    quarter = w_down.shape[1]
    topk_width = routing.shape[1]
    slot_rows = token_rows * topk_width // (owned_experts * devices)
    blocks = owned_experts + 1
    lane_rows = devices * slot_rows
    piece_rows = quarter // devices
    home_slots = targets(routing, replica, host_expert, owned_experts, devices, slot_rows, 1)
    home_matches, home_picker = selector(home_slots, blocks * lane_rows)
    row_x, row_dy, row_gate = fill_rows(home_matches, home_picker, tokens, grad_out, gates)
    sent_x, sent_dy, sent_gate = (
        lax.all_to_all(
            row_x.reshape(blocks, lane_rows, features),
            "expert",
            split_axis=1,
            concat_axis=1,
            tiled=True,
        ),
        lax.all_to_all(
            row_dy.reshape(blocks, lane_rows, features),
            "expert",
            split_axis=1,
            concat_axis=1,
            tiled=True,
        ),
        lax.all_to_all(
            row_gate.reshape(blocks, lane_rows), "expert", split_axis=1, concat_axis=1, tiled=True
        ),
    )
    block_x, block_dy, block_gate = (
        lax.all_gather(sent_x, "dp", axis=1, tiled=True),
        lax.all_gather(sent_dy, "dp", axis=1, tiled=True),
        lax.all_gather(sent_gate, "dp", axis=1, tiled=True),
    )
    owner_of_helper = host_expert // owned_experts
    owns_copy = owner_of_helper == device_id
    copied_local = jnp.sum(jnp.where(owns_copy, host_expert % owned_experts, 0))
    helper_ids = lax.broadcasted_iota(jnp.int32, (devices, devices), 1)
    owner_ids = lax.broadcasted_iota(jnp.int32, (devices, devices), 0)
    helper_of_owner = jnp.sum(
        jnp.where(owner_of_helper[None, :] == owner_ids, helper_ids, 0), axis=1
    )
    source_gu = lax.dynamic_index_in_dim(w_gate_up, copied_local, 0, keepdims=False)
    source_down = lax.dynamic_index_in_dim(w_down, copied_local, 0, keepdims=False)
    spread_gu, spread_down = (
        lax.all_to_all(
            source_gu.reshape(2, devices, piece_rows, features),
            "expert",
            split_axis=1,
            concat_axis=1,
            tiled=True,
        ),
        lax.all_to_all(
            source_down.reshape(1, devices, piece_rows, features),
            "expert",
            split_axis=1,
            concat_axis=1,
            tiled=True,
        ),
    )
    spread_gu = jnp.take(spread_gu, owner_of_helper, axis=1)
    spread_down = jnp.take(spread_down, owner_of_helper, axis=1)
    hosted_gu, hosted_down = (
        lax.all_to_all(spread_gu, "expert", split_axis=1, concat_axis=1, tiled=True),
        lax.all_to_all(spread_down, "expert", split_axis=1, concat_axis=1, tiled=True),
    )
    hosted_gu = hosted_gu.reshape(2, quarter, features)
    hosted_down = hosted_down.reshape(quarter, features)
    input_parts = []
    gate_parts = []
    owner_gu = []
    owner_down = []
    for block in range(blocks):
        if block < owned_experts:
            gate_up = w_gate_up[block]
            down_matrix = w_down[block]
        else:
            gate_up = hosted_gu
            down_matrix = hosted_down
        input_part, gate_part, weight_gu, weight_down = expert_block(
            block_x[block], block_dy[block], block_gate[block], gate_up, down_matrix
        )
        input_parts.append(input_part.astype(jnp.bfloat16))
        gate_parts.append(gate_part.astype(jnp.bfloat16))
        owner_gu.append(weight_gu)
        owner_down.append(weight_down)
    helper_gu = owner_gu[owned_experts].astype(jnp.bfloat16)
    helper_down = owner_down[owned_experts].astype(jnp.bfloat16)
    back_gu, back_down = (
        lax.all_to_all(
            helper_gu.reshape(2, devices, piece_rows, features),
            "expert",
            split_axis=1,
            concat_axis=1,
            tiled=True,
        ),
        lax.all_to_all(
            helper_down.reshape(1, devices, piece_rows, features),
            "expert",
            split_axis=1,
            concat_axis=1,
            tiled=True,
        ),
    )
    back_gu = jnp.take(back_gu, helper_of_owner, axis=1)
    back_down = jnp.take(back_down, helper_of_owner, axis=1)
    extra_gu, extra_down = (
        lax.all_to_all(back_gu, "expert", split_axis=1, concat_axis=1, tiled=True),
        lax.all_to_all(back_down, "expert", split_axis=1, concat_axis=1, tiled=True),
    )
    extra_gu = extra_gu.reshape(2, quarter, features).astype(jnp.float32)
    extra_down = extra_down.reshape(quarter, features).astype(jnp.float32)
    stacked_dx = jnp.stack(input_parts, axis=0)
    stacked_dg = jnp.stack(gate_parts, axis=0)
    summed_dx, summed_dg = (
        lax.psum_scatter(stacked_dx, "dp", scatter_dimension=1, tiled=True).astype(jnp.float32),
        lax.psum_scatter(stacked_dg, "dp", scatter_dimension=1, tiled=True).astype(jnp.float32),
    )
    row_dx = summed_dx.astype(jnp.bfloat16)
    row_dg = summed_dg.astype(jnp.bfloat16)
    home_dx, home_dg = (
        lax.all_to_all(row_dx, "expert", split_axis=1, concat_axis=1, tiled=True),
        lax.all_to_all(row_dg, "expert", split_axis=1, concat_axis=1, tiled=True),
    )
    home_dx = home_dx.reshape(blocks * lane_rows, features)
    home_dg = home_dg.reshape(blocks * lane_rows).astype(jnp.float32)
    grad_tokens = jnp.einsum(
        "st,sd->td", home_picker, home_dx, preferred_element_type=jnp.float32
    ).astype(jnp.bfloat16)
    grad_gates = jnp.sum(jnp.where(home_matches, home_dg[:, None, None], 0.0), axis=0)
    grad_gu = []
    grad_down = []
    for block in range(owned_experts):
        present = (copied_local == block).astype(jnp.float32)
        grad_gu.append((owner_gu[block] + present * extra_gu).astype(jnp.bfloat16))
        grad_down.append((owner_down[block] + present * extra_down).astype(jnp.bfloat16))
    return (grad_tokens, grad_gates, jnp.stack(grad_gu, axis=0), jnp.stack(grad_down, axis=0))


def solution(mesh):
    in_specs = (
        P(("dp", "expert"), None),
        P(("dp", "expert"), None),
        P(("dp", "expert"), None),
        P(("dp", "expert"), None),
        P(("dp", "expert"), None),
        P(),
        P("expert", None, "dp", None),
        P("expert", "dp", None),
    )
    out_specs = (
        P(("dp", "expert"), None),
        P(("dp", "expert"), None),
        P("expert", None, "dp", None),
        P("expert", "dp", None),
    )
    return jax.shard_map(shards, mesh=mesh, in_specs=in_specs, out_specs=out_specs, check_vma=False)
```

profile of v0, /device:TPU:0, one launch (start us, length us, event | category | flops | bytes accessed | tf_op | source)
XLA Modules:
  0.0 546.3 jit_solution(6755420541427667318)
XLA Ops:
  13.0 55.2 %all_to_all.73 = bf16[3,128,2048]{2,0,1:T(4,128)(2,1)S(1)} all-to-all(bf16[3,128,2048]{2,0,1:T(4,128)(2,1)S(1)} %copy.113), channel_id=1, replica_groups=mesh['dp'=4,'expert'=8] {'expert'}, dimensions={1} | all-to-all | bytes 3145728 | tf_op jit(solution)/shard_map/all_to_all | solution.py:93
  72.5 51.5 %all_to_all.74 = bf16[3,128,2048]{2,0,1:T(4,128)(2,1)S(1)} all-to-all(bf16[3,128,2048]{2,0,1:T(4,128)(2,1)S(1)} %copy.111), channel_id=1, replica_groups=mesh['dp'=4,'expert'=8] {'expert'}, dimensions={1} | all-to-all | bytes 3145728 | tf_op jit(solution)/shard_map/all_to_all | solution.py:100
  130.4 3.7 all-to-all-start.5
  135.1 36.7 %all-to-all-done.5 = bf16[2,8,24,2048]{3,2,0,1:T(8,128)(2,1)S(1)} async-done(((bf16[2,8,24,2048]{3,2,0,1:T(8,128)(2,1)}), bf16[2,8,24,2048]{3,2,0,1:T(8,128)(2,1)S(1)}, u32[]{:S(2)}, u32[]{:S(2)}) %all-to-all-start.5) | async-done | bytes 1572896 | tf_op jit(solution)/shard_map/all_to_all | solution.py:127
  171.8 4.2 all-to-all-start.3
  178.2 18.7 %all-to-all-done.3 = bf16[1,8,24,2048]{3,2,0,1:T(8,128)(2,1)} async-done(((bf16[1,8,24,2048]{3,2,0,1:T(8,128)(2,1)}), bf16[1,8,24,2048]{3,2,0,1:T(8,128)(2,1)}, u32[]{:S(2)}, u32[]{:S(2)}) %all-to-all-start.3) | async-done | bytes 786464 | tf_op jit(solution)/shard_map/all_to_all | solution.py:134
  197.0 3.6 all-to-all-start.6
  203.4 34.9 %all-to-all-done.6 = bf16[2,8,24,2048]{3,2,0,1:T(8,128)(2,1)S(1)} async-done(((bf16[2,8,24,2048]{3,2,0,1:T(8,128)(2,1)}), bf16[2,8,24,2048]{3,2,0,1:T(8,128)(2,1)S(1)}, u32[]{:S(2)}, u32[]{:S(2)}) %all-to-all-start.6) | async-done | bytes 1572896 | tf_op jit(solution)/shard_map/all_to_all | solution.py:145
  238.3 4.2 all-to-all-start.4
  245.7 17.8 %all-to-all-done.4 = bf16[1,8,24,2048]{3,2,0,1:T(8,128)(2,1)} async-done(((bf16[1,8,24,2048]{3,2,0,1:T(8,128)(2,1)}), bf16[1,8,24,2048]{3,2,0,1:T(8,128)(2,1)}, u32[]{:S(2)}, u32[]{:S(2)}) %all-to-all-start.4) | async-done | bytes 786464 | tf_op jit(solution)/shard_map/all_to_all | solution.py:146
  263.5 2.8 fusion.8
  266.3 3.2 fusion.35
  271.7 2.6 fusion.38
  277.4 23.2 %reduce-scatter.7.cloned.1.call-done = bf16[128,3]{1,0:T(8,128)(2,1)} async-done(((bf16[512,3]{1,0:T(8,128)(2,1)}), bf16[128,3]{1,0:T(8,128)(2,1)}) %reduce-scatter.7.cloned.1.call-update) | async-done | bytes 784
  302.1 4.6 all-to-all-start.8
  308.1 4.0 all-to-all-done.8
  317.0 8.0 %all_to_all.75 = bf16[3,8,16]{2,0,1:T(4,128)(2,1)S(1)} all-to-all(bf16[3,8,16]{2,0,1:T(4,128)(2,1)S(1)} %copy.109), channel_id=1, replica_groups=mesh['dp'=4,'expert'=8] {'expert'}, dimensions={1} | all-to-all | bytes 1536 | tf_op jit(solution)/shard_map/all_to_all | solution.py:107
  325.1 8.2 %all_gather.9 = bf16[3,512]{1,0:T(4,128)(2,1)S(1)} all-gather(bf16[3,128]{1,0:T(4,128)(2,1)S(1)} %all_to_all.46), channel_id=1, replica_groups=mesh['dp'=4,'expert'=8] {'dp'}, dimensions={1}, use_global_device_ids=true | all-gather | bytes 3840 | tf_op jit(solution)/shard_map/all_gather | solution.py:114
  333.4 2.9 fusion.99
  344.3 3.2 pad_maximum_fusion
  348.5 3.2 convolution_convert_fusion.3
  351.7 3.5 all-to-all-start.11
  359.1 17.0 %all-to-all-done.11 = bf16[1,8,24,2048]{3,2,0,1:T(8,128)(2,1)S(1)} async-done(((bf16[1,8,24,2048]{3,2,0,1:T(8,128)(2,1)}), bf16[1,8,24,2048]{3,2,0,1:T(8,128)(2,1)S(1)}, u32[]{:S(2)}, u32[]{:S(2)}) %all-to-all-start.11) | async-done | bytes 786464 | tf_op jit(solution)/shard_map/all_to_all | solution.py:178
  376.1 3.6 all-to-all-start.9
  381.5 35.9 %all-to-all-done.9 = bf16[2,8,24,2048]{3,2,0,1:T(8,128)(2,1)S(1)} async-done(((bf16[2,8,24,2048]{3,2,0,1:T(8,128)(2,1)}), bf16[2,8,24,2048]{3,2,0,1:T(8,128)(2,1)S(1)}, u32[]{:S(2)}, u32[]{:S(2)}) %all-to-all-start.9) | async-done | bytes 1572896 | tf_op jit(solution)/shard_map/all_to_all | solution.py:171
  417.4 4.2 all-to-all-start.12
  423.8 18.8 %all-to-all-done.12 = bf16[1,8,24,2048]{3,2,0,1:T(8,128)(2,1)} async-done(((bf16[1,8,24,2048]{3,2,0,1:T(8,128)(2,1)}), bf16[1,8,24,2048]{3,2,0,1:T(8,128)(2,1)}, u32[]{:S(2)}, u32[]{:S(2)}) %all-to-all-start.12) | async-done | bytes 786464 | tf_op jit(solution)/shard_map/all_to_all | solution.py:190
  442.6 3.6 all-to-all-start.10
  448.1 4.1 copy.119
  452.2 31.7 %all-to-all-done.10 = bf16[2,8,24,2048]{3,2,0,1:T(8,128)(2,1)S(1)} async-done(((bf16[2,8,24,2048]{3,2,0,1:T(8,128)(2,1)}), bf16[2,8,24,2048]{3,2,0,1:T(8,128)(2,1)S(1)}, u32[]{:S(2)}, u32[]{:S(2)}) %all-to-all-start.10) | async-done | bytes 1572896 | tf_op jit(solution)/shard_map/all_to_all | solution.py:189
  485.0 3.9 all-to-all-start.7
  504.2 33.4 %all-to-all-done.7 = bf16[3,128,2048]{2,0,1:T(4,128)(2,1)S(1)} async-done(((bf16[3,128,2048]{2,0,1:T(4,128)(2,1)}), bf16[3,128,2048]{2,0,1:T(4,128)(2,1)S(1)}, u32[]{:S(2)}, u32[]{:S(2)}) %all-to-all-start.7) | async-done | bytes 1572896 | tf_op jit(solution)/shard_map/all_to_all | solution.py:203
  (171 shorter events, 72.3 us)
Async XLA Ops:
  7.2 3.9 copy-start
  7.2 235.8 %all-gather.5.cloned.1.call-start = ((), (), s32[]{:S(2)}) async-start(), calls=%async_computation.16 | async-start | bytes 7864320 | tf_op jit(solution)/shard_map/all_gather | solution.py:112
  11.0 59.5 %copy-start.12 = (bf16[384,32]{0,1:T(8,128)(2,1)}, bf16[384,32]{0,1:T(8,128)(2,1)S(1)}, u32[]{:S(2)}) copy-start(bf16[384,32]{0,1:T(8,128)(2,1)S(1)} %convert_reduce_fusion) | copy-start | bytes 73732
  68.2 2.4 copy-start.24
  70.5 193.0 %all-gather.3.cloned.1.call-start = ((), (), s32[]{:S(2)}) async-start(), calls=%async_computation.15 | async-start | bytes 7864320 | tf_op jit(solution)/shard_map/all_gather | solution.py:113
  124.0 4.9 copy-start.4
  126.3 4.0 copy-start.27
  130.4 3.7 copy-start.9
  130.4 41.4 %all-to-all-start.5 = ((bf16[2,8,24,2048]{3,2,0,1:T(8,128)(2,1)}), bf16[2,8,24,2048]{3,2,0,1:T(8,128)(2,1)S(1)}, u32[]{:S(2)}, u32[]{:S(2)}) async-start(bf16[2,8,24,2048]{3,2,0,1:T(8,128)(2,1)} %copy.116), calls=%async_computation.5 | async-start | bytes 3145728 | tf_op jit(solution)/shard_map/all_to_all | solution.py:127
  171.8 25.2 %all-to-all-start.3 = ((bf16[1,8,24,2048]{3,2,0,1:T(8,128)(2,1)}), bf16[1,8,24,2048]{3,2,0,1:T(8,128)(2,1)}, u32[]{:S(2)}, u32[]{:S(2)}) async-start(bf16[1,8,24,2048]{3,2,0,1:T(8,128)(2,1)} %bitcast.30), calls=%async_computation.3 | async-start | bytes 1572864 | tf_op jit(solution)/shard_map/all_to_all | solution.py:134
  197.0 41.3 %all-to-all-start.6 = ((bf16[2,8,24,2048]{3,2,0,1:T(8,128)(2,1)}), bf16[2,8,24,2048]{3,2,0,1:T(8,128)(2,1)S(1)}, u32[]{:S(2)}, u32[]{:S(2)}) async-start(bf16[2,8,24,2048]{3,2,0,1:T(8,128)(2,1)} %select_bitcast_fusion.1), calls=%async_computation.6 | async-start | bytes 3145728 | tf_op jit(solution)/shard_map/all_to_all | solution.py:145
  238.3 25.2 %all-to-all-start.4 = ((bf16[1,8,24,2048]{3,2,0,1:T(8,128)(2,1)}), bf16[1,8,24,2048]{3,2,0,1:T(8,128)(2,1)}, u32[]{:S(2)}, u32[]{:S(2)}) async-start(bf16[1,8,24,2048]{3,2,0,1:T(8,128)(2,1)} %fusion.42), calls=%async_computation.4 | async-start | bytes 1572864 | tf_op jit(solution)/shard_map/all_to_all | solution.py:146
  242.5 58.2 %reduce-scatter.7.cloned.1.call-start = ((), (), s32[]{:S(2)}) async-start(), calls=%async_computation.18 | async-start | bytes 163840
  245.7 20.6 %copy-start.22 = (bf16[1,512,192]{1,2,0:T(8,128)(2,1)}, bf16[1,512,192]{1,2,0:T(8,128)(2,1)S(1)}, u32[]{:S(2)}) copy-start(bf16[1,512,192]{1,2,0:T(8,128)(2,1)S(1)} %multiply_convert_fusion) | copy-start | bytes 589828
  263.5 6.2 %slice-start.2 = ((s8[6291456]{0:T(1024)(128)(4,1)}), s8[4194304]{0:T(1024)(128)(4,1)S(1)}, s32[]{:S(2)}) async-start(s8[6291456]{0:T(1024)(128)(4,1)} %bitcast.321), calls=%async_computation.21 | async-start | bytes 8388608
  266.3 3.4 slice-start.3
  266.3 3.4 copy-start.10
  302.1 10.0 %all-to-all-start.8 = ((bf16[3,8,16]{2,0,1:T(4,128)(2,1)}), bf16[3,8,16]{2,0,1:T(4,128)(2,1)}, u32[]{:S(2)}, u32[]{:S(2)}) async-start(bf16[3,8,16]{2,0,1:T(4,128)(2,1)} %copy.121), calls=%async_computation.9 | async-start | bytes 16384 | tf_op jit(solution)/shard_map/all_to_all | solution.py:204
  306.7 141.4 %reduce-scatter.5.cloned.1.call-start = ((), (), s32[]{:S(2)}) async-start(), calls=%async_computation.17 | async-start | bytes 7864320 | tf_op jit(solution)/shard_map/reduce_scatter | solution.py:197
  333.4 4.3 slice-start.4
  336.4 2.4 copy-start.11
  348.5 6.8 %copy-start.30 = (bf16[1,512,192]{1,2,0:T(8,128)(2,1)S(1)}, bf16[1,512,192]{1,2,0:T(8,128)(2,1)}, u32[]{:S(2)}) copy-start(bf16[1,512,192]{1,2,0:T(8,128)(2,1)} %copy-done.29) | copy-start | bytes 589828
  348.5 6.8 %copy-start.32 = (bf16[1,512,192]{1,2,0:T(8,128)(2,1)S(1)}, bf16[1,512,192]{1,2,0:T(8,128)(2,1)}, u32[]{:S(2)}) copy-start(bf16[1,512,192]{1,2,0:T(8,128)(2,1)} %copy-done.31) | copy-start | bytes 589828
  351.7 24.4 %all-to-all-start.11 = ((bf16[1,8,24,2048]{3,2,0,1:T(8,128)(2,1)}), bf16[1,8,24,2048]{3,2,0,1:T(8,128)(2,1)S(1)}, u32[]{:S(2)}, u32[]{:S(2)}) async-start(bf16[1,8,24,2048]{3,2,0,1:T(8,128)(2,1)} %bitcast.61), calls=%async_computation.12 | async-start | bytes 1572864 | tf_op jit(solution)/shard_map/all_to_all | solution.py:178
  359.1 20.6 %copy-start.28 = (s32[8]{0:T(128)S(1)}, s32[8]{0:T(128)}, u32[]{:S(2)}) copy-start(s32[8]{0:T(128)} %copy-done.27) | copy-start | bytes 100
  376.1 41.3 %all-to-all-start.9 = ((bf16[2,8,24,2048]{3,2,0,1:T(8,128)(2,1)}), bf16[2,8,24,2048]{3,2,0,1:T(8,128)(2,1)S(1)}, u32[]{:S(2)}, u32[]{:S(2)}) async-start(bf16[2,8,24,2048]{3,2,0,1:T(8,128)(2,1)} %copy.123), calls=%async_computation.10 | async-start | bytes 3145728 | tf_op jit(solution)/shard_map/all_to_all | solution.py:171
  417.4 25.2 %all-to-all-start.12 = ((bf16[1,8,24,2048]{3,2,0,1:T(8,128)(2,1)}), bf16[1,8,24,2048]{3,2,0,1:T(8,128)(2,1)}, u32[]{:S(2)}, u32[]{:S(2)}) async-start(bf16[1,8,24,2048]{3,2,0,1:T(8,128)(2,1)} %fusion.41), calls=%async_computation.13 | async-start | bytes 1572864 | tf_op jit(solution)/shard_map/all_to_all | solution.py:190
  423.8 23.6 %copy-start.25 = (f32[32,8]{1,0:T(8,128)S(1)}, f32[32,8]{1,0:T(8,128)}, u32[]{:S(2)}) copy-start(f32[32,8]{1,0:T(8,128)} %get-tuple-element.14) | copy-start | bytes 3076
  442.6 41.3 %all-to-all-start.10 = ((bf16[2,8,24,2048]{3,2,0,1:T(8,128)(2,1)}), bf16[2,8,24,2048]{3,2,0,1:T(8,128)(2,1)S(1)}, u32[]{:S(2)}, u32[]{:S(2)}) async-start(bf16[2,8,24,2048]{3,2,0,1:T(8,128)(2,1)} %select_bitcast_fusion), calls=%async_computation.11 | async-start | bytes 3145728 | tf_op jit(solution)/shard_map/all_to_all | solution.py:189
  485.0 52.6 %all-to-all-start.7 = ((bf16[3,128,2048]{2,0,1:T(4,128)(2,1)}), bf16[3,128,2048]{2,0,1:T(4,128)(2,1)S(1)}, u32[]{:S(2)}, u32[]{:S(2)}) async-start(bf16[3,128,2048]{2,0,1:T(4,128)(2,1)} %copy.119), calls=%async_computation.8 | async-start | bytes 4194304 | tf_op jit(solution)/shard_map/all_to_all | solution.py:203
  502.2 37.6 %copy-start.1 = (bf16[32,2048]{1,0:T(8,128)(2,1)S(1)}, bf16[32,2048]{1,0:T(8,128)(2,1)}, u32[]{:S(2)}) copy-start(bf16[32,2048]{1,0:T(8,128)(2,1)} %param.12) | copy-start | bytes 393220
  504.2 34.6 %copy-start.13 = (bf16[384,32]{0,1:T(8,128)(2,1)S(1)}, bf16[384,32]{0,1:T(8,128)(2,1)}, u32[]{:S(2)}) copy-start(bf16[384,32]{0,1:T(8,128)(2,1)} %copy-done.12) | copy-start | bytes 73732
  (21 other events, 34.9 us)
Sparse Core Ops, SparseCore 0:
  70.6 68.9 all-gather.4
  141.4 70.0 all-gather.2
  277.6 23.0 reduce-scatter.6
  347.7 67.2 reduce-scatter.4
where the time goes:
time: 548 us; the launch traced here: 546 us
  waiting for transfers between devices  272 us (50%)
  blocking collectives  123 us (22%)
  starting transfers between devices  39.4 us (7%)
  matrix products  36.4 us (7%)
  local copies, waits for them, and re-layouts  35.9 us (7%)
  other arithmetic  21.5 us (4%)
  between operations  17.8 us (3%)
    all_to_all x1, blocking collectives, shards(): lax.all_to_all(row_x.reshape(blocks, lane_rows, features), 'expert', spli...  55.2 us
    all_to_all x1, blocking collectives, shards(): lax.all_to_all(row_dy.reshape(blocks, lane_rows, features), 'expert', spl...  51.5 us
    all_to_all x1, waiting for transfers between devices, shards(): lax.all_to_all(source_gu.reshape(2, devices, piece_rows, features), 'expe...  36.7 us
    all_to_all x1, waiting for transfers between devices, shards(): lax.all_to_all(helper_gu.reshape(2, devices, piece_rows, features), 'expe...  35.9 us
    all_to_all x1, waiting for transfers between devices, shards(): lax.all_to_all(spread_gu, 'expert', split_axis=1, concat_axis=1, tiled=True)  34.9 us
    all_to_all x1, waiting for transfers between devices, shards(): lax.all_to_all(row_dx, 'expert', split_axis=1, concat_axis=1, tiled=True)  33.4 us
    all_to_all x1, waiting for transfers between devices, shards(): lax.all_to_all(back_gu, 'expert', split_axis=1, concat_axis=1, tiled=True)  31.7 us
    unnamed x5, waiting for transfers between devices  23.3 us
  transfers between devices with their start and end apart: 14, of which 11 were waited for; matrix products, arithmetic and copies ran while one was open for 8% of the time, Pallas kernels for 0%

commit v1 on v0

--- a/solution.py
+++ b/solution.py
@@ -218,6 +218,73 @@
     return (grad_tokens, grad_gates, jnp.stack(grad_gu, axis=0), jnp.stack(grad_down, axis=0))
 
 
+def chosen_gates(routing, replica, gates, host_expert, experts):
+    listed = jnp.any(routing[:, :, None] == host_expert[None, None, :], axis=2)
+    usable = (replica == 0) | listed
+    picks = usable[:, :, None] & (
+        routing[:, :, None] == lax.broadcasted_iota(jnp.int32, routing.shape + (experts,), 2)
+    )
+    weights = jnp.sum(jnp.where(picks, gates.astype(jnp.float32)[:, :, None], 0.0), axis=1)
+    return (picks, weights)
+
+
+def gathered_shards(
+    tokens, grad_out, routing, replica, gates, host_expert, w_gate_up, w_down
+):
+    devices = lax.axis_size("expert")
+    device_id = lax.axis_index("expert")
+    rows, features = tokens.shape
+    owned = w_gate_up.shape[0]
+    experts = owned * devices
+    lanes = (experts + 127) // 128 * 128
+    picks, weights = chosen_gates(routing, replica, gates, host_expert, experts)
+    side = jnp.pad(weights.astype(jnp.bfloat16), ((0, 0), (0, lanes - experts)))
+    payload = jnp.concatenate([tokens, grad_out, side], axis=1)
+    payload = lax.all_gather(payload, ("dp", "expert"), axis=0, tiled=True)
+    every_x = payload[:, :features]
+    every_dy = payload[:, features : 2 * features]
+    own_gates = lax.dynamic_slice_in_dim(
+        payload[:, 2 * features : 2 * features + experts], device_id * owned, owned, axis=1
+    ).astype(jnp.float32)
+    mixed = jnp.einsum("td,ejfd->jtef", every_x, w_gate_up, preferred_element_type=jnp.float32)
+    raw_hidden = jnp.einsum("td,efd->tef", every_dy, w_down, preferred_element_type=jnp.float32)
+    gate_pre = mixed[0]
+    up_part = mixed[1]
+    sigmoid_gate = jax.nn.sigmoid(gate_pre)
+    active = gate_pre * sigmoid_gate
+    hidden = (active * up_part).astype(jnp.bfloat16).astype(jnp.float32)
+    gate_part = jnp.sum(hidden * raw_hidden, axis=2)
+    weighted = (hidden * own_gates[:, :, None]).astype(jnp.bfloat16)
+    grad_hidden = raw_hidden * own_gates[:, :, None]
+    grad_gate = grad_hidden * up_part * sigmoid_gate * (1.0 + gate_pre * (1.0 - sigmoid_gate))
+    grad_mixed = jnp.stack([grad_gate, grad_hidden * active], axis=0).astype(jnp.bfloat16)
+    input_part = jnp.einsum(
+        "jtef,ejfd->td", grad_mixed, w_gate_up, preferred_element_type=jnp.float32
+    ).astype(jnp.bfloat16)
+    slots = lax.broadcasted_iota(jnp.int32, (owned, lanes), 1)
+    starts = device_id * owned + lax.broadcasted_iota(jnp.int32, (owned, lanes), 0)
+    gate_side = jnp.sum(
+        jnp.where((slots == starts)[None], gate_part[:, :, None], 0.0), axis=1
+    ).astype(jnp.bfloat16)
+    partial = jnp.concatenate([input_part, gate_side], axis=1)
+    summed = lax.psum_scatter(partial, ("dp", "expert"), scatter_dimension=0, tiled=True)
+    grad_gu = jnp.einsum(
+        "jtef,td->ejfd", grad_mixed, every_x, preferred_element_type=jnp.float32
+    ).astype(jnp.bfloat16)
+    grad_down = jnp.einsum(
+        "tef,td->efd", weighted, every_dy, preferred_element_type=jnp.float32
+    ).astype(jnp.bfloat16)
+    grad_tokens = summed[:, :features]
+    sums = summed[:, features : features + experts].astype(jnp.float32)
+    grad_gates = jnp.sum(jnp.where(picks, sums[:, None, :], 0.0), axis=2)
+    return (grad_tokens, grad_gates, grad_gu, grad_down)
+
+
+def serve(tokens, grad_out, routing, replica, gates, host_expert, w_gate_up, w_down):
+    body = gathered_shards if routing.shape[1] >= lax.axis_size("expert") else shards
+    return body(tokens, grad_out, routing, replica, gates, host_expert, w_gate_up, w_down)
+
+
 def solution(mesh):
     in_specs = (
         P(("dp", "expert"), None),
@@ -235,4 +302,4 @@
         P("expert", None, "dp", None),
         P("expert", "dp", None),
     )
-    return jax.shard_map(shards, mesh=mesh, in_specs=in_specs, out_specs=out_specs, check_vma=False)
+    return jax.shard_map(serve, mesh=mesh, in_specs=in_specs, out_specs=out_specs, check_vma=False)

time: 548 us -> 266 us (0.49)
  blocking collectives: 123 us -> 0 us
  waiting for transfers between devices: 272 us -> 210 us
  starting transfers between devices: 39.4 us -> 0.08 us
  local copies, waits for them, and re-layouts: 35.9 us -> 6.39 us
  matrix products: 36.4 us -> 25.1 us
  other arithmetic: 21.5 us -> 10.3 us
    all_to_all x10 -> x0, waiting for transfers between devices: 249 us -> none  [the longest x1 36.7 us: shards(): lax.all_to_all(source_gu.reshape(2, devices, piece_rows, features), 'expe...]
    all_to_all x3 -> x0, blocking collectives: 115 us -> none  [the longest x1 55.2 us: shards(): lax.all_to_all(row_x.reshape(blocks, lane_rows, features), 'expert', spli...]
    unnamed x5 -> x3, waiting for transfers between devices: 23.3 us -> 129 us
    all_gather x2 -> x1, waiting for transfers between devices: 0.02 us -> 80.9 us  [gathered_shards(): payload = lax.all_gather(payload, ('dp', 'expert'), axis=0, tiled=True)]
    all_to_all x10 -> x0, starting transfers between devices: 39.1 us -> none  [the longest x1 4.59 us: shards(): lax.all_to_all(row_dg, 'expert', split_axis=1, concat_axis=1, tiled=True)]
    dot_general x21 -> x4, matrix products: 36.4 us -> 19.8 us  [the longest x1 5.55 us: gathered_shards(): jnp.einsum('td,efd->tef', every_dy, w_down, preferred_element_type=jnp.fl...]
    all_gather x1 -> x0, blocking collectives: 8.25 us -> none  [shards(): lax.all_gather(sent_gate, 'dp', axis=1, tiled=True)]
    all_to_all x9 -> x0, local copies, waits for them, and re-layouts: 7.77 us -> none  [the longest x1 2.29 us: shards(): lax.all_to_all(row_dy.reshape(blocks, lane_rows, features), 'expert', spl...]
  transfers between devices with their start and end apart: 14 -> 2, of which waited for: 11 -> 2; matrix products, arithmetic and copies ran while one was open for 8% -> 5% of each run, Pallas kernels for 0% -> 0%
where the time goes in v1:
time: 266 us
  waiting for transfers between devices  210 us (79%)
  matrix products  25.1 us (9%)
  between operations  14.2 us (5%)
  other arithmetic  10.3 us (4%)
  local copies, waits for them, and re-layouts  6.39 us (2%)
    unnamed x3, waiting for transfers between devices  129 us
    all_gather x1, waiting for transfers between devices, gathered_shards(): payload = lax.all_gather(payload, ('dp', 'expert'), axis=0, tiled=True)  80.9 us
    dot_general x1, matrix products, gathered_shards(): jnp.einsum('td,efd->tef', every_dy, w_down, preferred_element_type=jnp.fl...  5.55 us
    dot_general x1, matrix products, gathered_shards(): jnp.einsum('td,ejfd->jtef', every_x, w_gate_up, preferred_element_type=jn...  5.38 us
  transfers between devices with their start and end apart: 2, of which 2 were waited for; matrix products, arithmetic and copies ran while one was open for 5% of the time, Pallas kernels for 0%

profile of v1, /device:TPU:0, one launch (start us, length us, event | category | flops | bytes accessed | tf_op | source)
XLA Modules:
  0.0 265.8 jit_solution(7489028899461557723)
XLA Ops:
  7.2 0.0 all-gather.2.cloned.1.call-start
  7.2 0.8 convert_element_type.39
  8.1 0.8 compare_reduce_fusion
  8.9 0.7 compare_or_fusion
  9.6 0.7 select_reduce_fusion.2
  10.3 0.1 copy.63
  10.4 1.7 fusion.23
  12.1 0.0 all-gather.2.cloned.1.call-update
  12.1 0.0 reduce-scatter.4.cloned.1.call-start
  12.2 0.1 iota_compare_fusion.2
  12.3 80.9 %all-gather.2.cloned.1.call-done = bf16[1024,4224]{1,0:T(8,128)(2,1)} async-done(((bf16[32,4224]{1,0:T(8,128)(2,1)}), bf16[1024,4224]{1,0:T(8,128)(2,1)}) %all-gather.2.cloned.1.call-update) | async-done | bytes 8650768 | tf_op jit(solution)/shard_map/all_gather | solution.py:243
  93.2 1.0 slice.29
  94.1 0.1 constant_dynamic-slice_fusion
  94.3 0.1 copy.60
  94.4 5.4 %fusion.9 = f32[2,1024,2,192]{1,3,2,0:T(8,128)S(1)} fusion(bf16[2,2,192,2048]{3,2,1,0:T(8,128)(2,1)S(1)} %copy-done, bf16[1024,4224]{1,0:T(8,128)(2,1)} %all-gather.2.cloned.1.call-done), kind=kOutput, calls=%fused_computation.15 | convolution fusion | flops 3221225472 | bytes 10485760 | tf_op jit(solution)/shard_map/td,ejfd->jtef/dot_general | solution.py:249
  99.8 5.6 %fusion.21 = (bf16[1,1024,2,192]{1,3,2,0:T(8,128)(2,1)S(1)}, bf16[1,1024,2,192]{1,3,2,0:T(8,128)(2,1)S(1)}, f32[1024,2]{0,1:T(2,128)S(1)}, bf16[1024,2,192]{0,2,1:T(8,128)(2,1)}) fusion(f32[2,1024,2,192]{1,3,2,0:T(8,128)S(1)} %fusion.9, f32[1024,2]{0,1:T(2,128)S(1)} %convert_element_type.41, bf16[2,192,2048]{2,1,0:T(8,128)(2,1)S(1)} %copy-done.4, ...), kind=kOutput, calls=%fused_computation.30 | convolution fusion | flops 1618081792 | bytes 11288576 | tf_op jit(solution)/shard_map/td,efd->tef/dot_general | solution.py:250
  105.4 0.3 select_reduce_fusion
  105.7 0.6 copy-done.1
  106.3 0.2 copy-done.2
  106.5 3.7 %bitcast_convert_fusion = bf16[1024,2048]{1,0:T(8,128)(2,1)S(1)} fusion(bf16[2,2,192,2048]{3,2,1,0:T(8,128)(2,1)S(1)} %copy-done, bf16[1,1024,2,192]{1,3,2,0:T(8,128)(2,1)S(1)} %get-tuple-element.27, bf16[1,1024,2,192]{1,3,2,0:T(8,128)(2,1)S(1)} %get-tuple-element.26), kind=kOutput, calls=%fused_computation | convolution fusion | flops 3224109056 | bytes 8912896 | tf_op jit(solution)/shard_map/jtef,ejfd->td/dot_general | solution.py:261
  110.2 2.5 pad_maximum_fusion
  112.7 0.0 reduce-scatter.4.cloned.1.call-update
  112.8 1.5 pad_maximum_fusion.1
  114.3 5.3 %fusion.2 = f32[2048,768]{0,1:S(1)} fusion(bf16[1024,768]{0,1:T(8,128)(2,1)S(1)} %bitcast.56, bf16[1024,4224]{1,0:T(8,128)(2,1)} %all-gather.2.cloned.1.call-done), kind=kOutput, calls=%fused_computation.5 | convolution fusion | flops 3221225472 | bytes 12058624
  119.5 0.5 convert_bitcast_fusion
  120.0 1.9 copy.53
  121.9 5.2 %fusion.8 = bf16[2,192,2048]{2,1,0:T(8,128)(2,1)} fusion(bf16[1024,4224]{1,0:T(8,128)(2,1)} %all-gather.2.cloned.1.call-done, bf16[1024,2,192]{0,2,1:T(8,128)(2,1)S(1)} %copy-done.5, f32[1024,2]{0,1:T(2,128)S(1)} %convert_element_type.41), kind=kOutput, calls=%fused_computation.12 | convolution fusion | flops 1612578816 | bytes 6561792 | tf_op jit(solution)/shard_map/tef,td->efd/dot_general | solution.py:274
  127.1 128.9 %reduce-scatter.4.cloned.1.call-done = bf16[32,2176]{1,0:T(8,128)(2,1)} async-done(((bf16[1024,2176]{1,0:T(8,128)(2,1)}), bf16[32,2176]{1,0:T(8,128)(2,1)}) %reduce-scatter.4.cloned.1.call-update) | async-done | bytes 139280
  256.0 0.7 slice.34
  256.7 0.1 copy.62
  256.7 0.6 select_reduce_fusion.1
  257.4 1.6 slice.33
  (13 shorter events, 0.0 us)
Async XLA Ops:
  7.2 87.3 %copy-start = (bf16[2,2,192,2048]{3,2,1,0:T(8,128)(2,1)S(1)}, bf16[2,2,192,2048]{3,2,1,0:T(8,128)(2,1)}, u32[]{:S(2)}) copy-start(bf16[2,2,192,2048]{3,2,1,0:T(8,128)(2,1)} %param.14) | copy-start | bytes 9437188
  7.2 86.0 %all-gather.2.cloned.1.call-start = ((), (), s32[]{:S(2)}) async-start(), calls=%async_computation.1 | async-start | bytes 8921088 | tf_op jit(solution)/shard_map/all_gather | solution.py:243
  12.1 243.8 %reduce-scatter.4.cloned.1.call-start = ((), (), s32[]{:S(2)}) async-start(), calls=%async_computation.2 | async-start | bytes 4595712
  94.4 5.4 %copy-start.4 = (bf16[2,192,2048]{2,1,0:T(8,128)(2,1)S(1)}, bf16[2,192,2048]{2,1,0:T(8,128)(2,1)}, u32[]{:S(2)}) copy-start(bf16[2,192,2048]{2,1,0:T(8,128)(2,1)} %param.15) | copy-start | bytes 4718596
  105.4 0.9 copy-start.1
  105.4 1.1 copy-start.2
  120.0 1.9 copy-start.5
  121.9 134.8 %copy-start.3 = (s32[32,8]{0,1:T(8,128)S(1)}, s32[32,8]{0,1:T(8,128)}, u32[]{:S(2)}) copy-start(s32[32,8]{0,1:T(8,128)} %param.10) | copy-start | bytes 3076
Sparse Core Ops, SparseCore 0:
  12.2 80.8 all-gather.1
  112.9 143.0 reduce-scatter.3

commit v2 on v1

--- a/solution.py
+++ b/solution.py
@@ -1,7 +1,13 @@
+import functools
+
 import jax
 import jax.numpy as jnp
 from jax import lax
+from jax.experimental import pallas as pl
+from jax.experimental.pallas import tpu as pltpu
 from jax.sharding import PartitionSpec as P
+
+MESH = pl.DeviceIdType.MESH
 
 
 def lookup(values_table, indices):
@@ -228,6 +234,271 @@
     return (picks, weights)
 
 
+def greet(partners):
+    barrier = pltpu.get_barrier_semaphore()
+    for condition, device in partners:
+
+        @pl.when(condition)
+        def _():
+            pl.semaphore_signal(barrier, inc=1, device_id=device, device_id_type=MESH)
+
+    pl.semaphore_wait(barrier, sum(condition.astype(jnp.int32) for condition, _ in partners))
+
+
+def place(depth):
+    dp = lax.axis_index("dp")
+    expert = lax.axis_index("expert")
+    height, core = expert // 2, expert % 2
+    row, column = dp // 2, dp % 2
+    across = row * 2 + 1 - column
+    along = (1 - row) * 2 + column
+    diagonal = (1 - row) * 2 + 1 - column
+    return dp, expert, height, core, across, along, diagonal
+
+
+def gather_kernel(depth, source, out, sent, landed, local):
+    dp, expert, height, core, across, along, diagonal = place(depth)
+    half = source.shape[0] // 2
+    partner = (dp, height * 2 + 1 - core)
+    x_device = (across, expert)
+    y_device = (along, expert)
+    up_device = (dp, jnp.minimum(expert + 2, 2 * depth - 1))
+    down_device = (dp, jnp.maximum(expert - 2, 0))
+    has_up = height < depth - 1
+    has_down = height > 0
+    always = height >= 0
+    greet(
+        [
+            (always, partner),
+            (always, x_device),
+            (always, y_device),
+            (has_up, up_device),
+            (has_down, down_device),
+        ]
+    )
+
+    def slot_of(dp_from, height_from, core_from):
+        return (dp_from * depth + height_from) * 2 + core_from
+
+    def copy(slot, way, device, part=None, own=False):
+        block = source if own else out.at[slot]
+        into = out.at[slot]
+        piece = 0
+        if part is not None:
+            block = block.at[pl.ds(part * half, half)]
+            into = into.at[pl.ds(part * half, half)]
+            piece = part
+        return pltpu.make_async_remote_copy(
+            src_ref=block,
+            dst_ref=into,
+            send_sem=sent.at[slot, way * 2 + piece],
+            recv_sem=landed.at[slot, piece],
+            device_id=device,
+            device_id_type=MESH,
+        )
+
+    finish = []
+
+    def send(condition, *args, **kwargs):
+        finish.append((condition, args, kwargs))
+        if condition is always:
+            copy(*args, **kwargs).start()
+        else:
+
+            @pl.when(condition)
+            def _():
+                copy(*args, **kwargs).start()
+
+    def arrive(condition, slot, part=None):
+        if condition is always:
+            copy(slot, 0, partner, part).wait_recv()
+        else:
+
+            @pl.when(condition)
+            def _():
+                copy(slot, 0, partner, part).wait_recv()
+
+    def both(first, second):
+        return first if second is always else jnp.logical_and(first, second)
+
+    mine = slot_of(dp, height, core)
+    send(has_up, mine, 3, up_device, own=True)
+    send(has_down, mine, 4, down_device, own=True)
+    send(always, mine, 1, x_device, own=True)
+    send(always, mine, 2, y_device, own=True)
+    send(always, mine, 0, partner, own=True)
+    keep = pltpu.make_async_copy(source, out.at[mine], local)
+    keep.start()
+    steps = [[(always, height)]]
+    for distance in range(1, depth):
+        steps.append([(height >= distance, jnp.maximum(height - distance, 0))])
+        steps[-1].append(
+            (height + distance < depth, jnp.minimum(height + distance, depth - 1))
+        )
+    for index in range(depth + 2):
+        if 0 < index < depth:
+            for side, (condition, level) in enumerate(steps[index]):
+                slot = slot_of(dp, level, core)
+                arrive(condition, slot)
+                if side == 0:
+                    send(both(condition, has_up), slot, 3, up_device)
+                else:
+                    send(both(condition, has_down), slot, 4, down_device)
+                send(condition, slot, 1, x_device)
+                send(condition, slot, 2, y_device)
+                send(condition, slot, 0, partner)
+        if 0 <= index - 1 < depth:
+            for condition, level in steps[index - 1]:
+                slot = slot_of(across, level, core)
+                arrive(condition, slot)
+                send(condition, slot, 2, y_device, part=0)
+                send(condition, slot, 0, partner)
+                slot = slot_of(along, level, core)
+                arrive(condition, slot)
+                send(condition, slot, 1, x_device, part=1)
+                send(condition, slot, 0, partner)
+        if 0 <= index - 2 < depth:
+            for condition, level in steps[index - 2]:
+                slot = slot_of(diagonal, level, core)
+                for part in range(2):
+                    arrive(condition, slot, part)
+                    send(condition, slot, 0, partner, part=part)
+    keep.wait()
+    for level in range(depth):
+        for dp_from in (dp, across, along):
+            arrive(always, slot_of(dp_from, level, 1 - core))
+        for part in range(2):
+            arrive(always, slot_of(diagonal, level, 1 - core), part)
+    for condition, args, kwargs in finish:
+        if condition is always:
+            copy(*args, **kwargs).wait_send()
+        else:
+
+            @pl.when(condition)
+            def _():
+                copy(*args, **kwargs).wait_send()
+
+
+def gather_rows(payload, dp_size, expert_size):
+    rows, width = payload.shape
+    depth = expert_size // 2
+    slots = dp_size * expert_size
+    out = pl.pallas_call(
+        functools.partial(gather_kernel, depth),
+        out_shape=jax.ShapeDtypeStruct((slots, rows, width), payload.dtype),
+        in_specs=[pl.BlockSpec(memory_space=pl.ANY)],
+        out_specs=pl.BlockSpec(memory_space=pl.ANY),
+        scratch_shapes=[
+            pltpu.SemaphoreType.DMA((slots, 10)),
+            pltpu.SemaphoreType.DMA((slots, 2)),
+            pltpu.SemaphoreType.DMA,
+        ],
+        compiler_params=pltpu.CompilerParams(collective_id=0, has_side_effects=True),
+    )(payload)
+    return out.reshape(slots * rows, width)
+
+
+def scatter_kernel(
+    depth, part_ref, out, paired, ready, crossed, column, risen, total, sems, landed
+):
+    dp, expert, height, core, across, along, diagonal = place(depth)
+    others = (across, along, diagonal)
+    partner = (dp, height * 2 + 1 - core)
+    levels = [lax.rem(height + step, depth) for step in range(1, depth)] + [height]
+    always = height >= 0
+    greet(
+        [(always, partner)]
+        + [(always, (other, expert)) for other in others]
+        + [(always, (dp, level * 2 + core)) for level in levels[:-1]]
+    )
+
+    def remote(block, into, index, device):
+        return pltpu.make_async_remote_copy(
+            src_ref=block,
+            dst_ref=into,
+            send_sem=sems.at[index],
+            recv_sem=landed.at[index],
+            device_id=device,
+            device_id_type=MESH,
+        )
+
+    def pair_copy(step):
+        return remote(part_ref.at[:, levels[step], 1 - core], paired.at[step], step, partner)
+
+    def cross_copy(step, way):
+        return remote(
+            ready.at[step, way],
+            crossed.at[step, way],
+            depth + step * 3 + way,
+            (others[way], expert),
+        )
+
+    def rise_copy(step):
+        return remote(
+            column.at[step], risen.at[step], 4 * depth + step, (dp, levels[step] * 2 + core)
+        )
+
+    for step in range(depth):
+        pair_copy(step).start()
+    for step in range(depth):
+        pair_copy(step).wait_recv()
+        for way in (2, 0, 1):
+            ready[step, way] = (
+                part_ref[others[way], levels[step], core].astype(jnp.float32)
+                + paired[step, others[way]].astype(jnp.float32)
+            ).astype(jnp.bfloat16)
+            cross_copy(step, way).start()
+    for step in range(depth):
+        for way in range(3):
+            cross_copy(step, way).wait_recv()
+        summed = part_ref[dp, levels[step], core].astype(jnp.float32) + paired[
+            step, dp
+        ].astype(jnp.float32)
+        for way in range(3):
+            summed = summed + crossed[step, way].astype(jnp.float32)
+        if step < depth - 1:
+            column[step] = summed.astype(jnp.bfloat16)
+            rise_copy(step).start()
+        else:
+            total[...] = summed
+    for step in range(depth - 1):
+        rise_copy(step).wait_recv()
+        total[...] = total[...] + risen[step].astype(jnp.float32)
+    out[...] = total[...].astype(jnp.bfloat16)
+    for step in range(depth):
+        pair_copy(step).wait_send()
+        for way in range(3):
+            cross_copy(step, way).wait_send()
+        if step < depth - 1:
+            rise_copy(step).wait_send()
+
+
+def scatter_rows(partial, dp_size, expert_size):
+    rows = partial.shape[0] // (dp_size * expert_size)
+    width = partial.shape[1]
+    depth = expert_size // 2
+    block = (rows, width)
+    return pl.pallas_call(
+        functools.partial(scatter_kernel, depth),
+        out_shape=jax.ShapeDtypeStruct(block, partial.dtype),
+        in_specs=[pl.BlockSpec(memory_space=pltpu.VMEM)],
+        out_specs=pl.BlockSpec(memory_space=pltpu.VMEM),
+        scratch_shapes=[
+            pltpu.VMEM((depth, dp_size) + block, jnp.bfloat16),
+            pltpu.VMEM((depth, 3) + block, jnp.bfloat16),
+            pltpu.VMEM((depth, 3) + block, jnp.bfloat16),
+            pltpu.VMEM((depth,) + block, jnp.bfloat16),
+            pltpu.VMEM((depth,) + block, jnp.bfloat16),
+            pltpu.VMEM(block, jnp.float32),
+            pltpu.SemaphoreType.DMA((5 * depth,)),
+            pltpu.SemaphoreType.DMA((5 * depth,)),
+        ],
+        compiler_params=pltpu.CompilerParams(
+            collective_id=1, has_side_effects=True, vmem_limit_bytes=48 << 20
+        ),
+    )(partial.reshape(dp_size, depth, 2, rows, width))
+
+
 def gathered_shards(
     tokens, grad_out, routing, replica, gates, host_expert, w_gate_up, w_down
 ):
@@ -240,7 +511,8 @@
     picks, weights = chosen_gates(routing, replica, gates, host_expert, experts)
     side = jnp.pad(weights.astype(jnp.bfloat16), ((0, 0), (0, lanes - experts)))
     payload = jnp.concatenate([tokens, grad_out, side], axis=1)
-    payload = lax.all_gather(payload, ("dp", "expert"), axis=0, tiled=True)
+    dp_size = lax.axis_size("dp")
+    payload = gather_rows(payload, dp_size, devices)
     every_x = payload[:, :features]
     every_dy = payload[:, features : 2 * features]
     own_gates = lax.dynamic_slice_in_dim(
@@ -267,7 +539,7 @@
         jnp.where((slots == starts)[None], gate_part[:, :, None], 0.0), axis=1
     ).astype(jnp.bfloat16)
     partial = jnp.concatenate([input_part, gate_side], axis=1)
-    summed = lax.psum_scatter(partial, ("dp", "expert"), scatter_dimension=0, tiled=True)
+    summed = scatter_rows(partial, dp_size, devices)
     grad_gu = jnp.einsum(
         "jtef,td->ejfd", grad_mixed, every_x, preferred_element_type=jnp.float32
     ).astype(jnp.bfloat16)
@@ -281,7 +553,9 @@
 
 
 def serve(tokens, grad_out, routing, replica, gates, host_expert, w_gate_up, w_down):
-    body = gathered_shards if routing.shape[1] >= lax.axis_size("expert") else shards
+    squares = lax.axis_size("dp") == 4 and lax.axis_size("expert") % 2 == 0
+    visits_all = routing.shape[1] >= lax.axis_size("expert")
+    body = gathered_shards if squares and visits_all else shards
     return body(tokens, grad_out, routing, replica, gates, host_expert, w_gate_up, w_down)
 
 

time: 266 us -> 110 us (0.41)
  waiting for transfers between devices: 210 us -> 0 us
  Pallas kernels: 0 us -> 78.3 us
  between operations: 14.2 us -> 0.82 us
  matrix products: 25.1 us -> 18.2 us
  other arithmetic: 10.3 us -> 6.79 us
    unnamed x3 -> x0, waiting for transfers between devices: 129 us -> none
    all_gather x1 -> x0, waiting for transfers between devices: 80.9 us -> none  [gathered_shards(): payload = lax.all_gather(payload, ('dp', 'expert'), axis=0, tiled=True)]
    pallas_call x0 -> x2, Pallas kernels: none -> 78.3 us  [the longest x1 47.5 us: gather_rows(): pl.pallas_call(functools.partial(gather_kernel, depth), out_shape=jax.Sha...]
    dot_general x1, matrix products: 5.55 us -> 2.72 us  [gathered_shards(): jnp.einsum('td,efd->tef', every_dy, w_down, preferred_element_type=jnp.fl...]
  transfers between devices with their start and end apart: 2 -> 0, of which waited for: 2 -> 0; matrix products, arithmetic and copies ran while one was open for 5% -> 0% of each run, Pallas kernels for 0% -> 0%
where the time goes in v2:
time: 110 us
  Pallas kernels  78.3 us (71%)
  matrix products  18.2 us (17%)
  other arithmetic  6.79 us (6%)
  local copies, waits for them, and re-layouts  5.83 us (5%)
    pallas_call x1, Pallas kernels, gather_rows(): pl.pallas_call(functools.partial(gather_kernel, depth), out_shape=jax.Sha...  47.5 us
    pallas_call x1, Pallas kernels, scatter_rows(): pl.pallas_call(functools.partial(scatter_kernel, depth), out_shape=jax.Sh...  30.8 us
    dot_general x1, matrix products, gathered_shards(): jnp.einsum('td,ejfd->jtef', every_x, w_gate_up, preferred_element_type=jn...  5.41 us
    dot_general x1, matrix products, gathered_shards(): jnp.einsum('jtef,ejfd->td', grad_mixed, w_gate_up, preferred_element_type...  3.71 us
    unnamed x1, matrix products  3.41 us
    unnamed x14, local copies, waits for them, and re-layouts  3.19 us
    dot_general x1, matrix products, gathered_shards(): jnp.einsum('tef,td->efd', weighted, every_dy, preferred_element_type=jnp....  2.95 us
    dot_general x1, matrix products, gathered_shards(): jnp.einsum('td,efd->tef', every_dy, w_down, preferred_element_type=jnp.fl...  2.72 us

profile of v2, /device:TPU:0, one launch (start us, length us, event | category | flops | bytes accessed | tf_op | source)
XLA Modules:
  0.0 110.0 jit_solution(11160280612573615403)
XLA Ops:
  0.6 0.0 copy-start
  0.7 0.1 iota_compare_fusion.2
  0.7 0.9 compare_reduce_fusion
  1.7 0.7 compare_or_fusion
  2.4 0.7 convert_element_type.39
  3.0 0.7 select_reduce_fusion.2
  3.8 0.1 copy.35
  3.8 1.7 %fusion.23.source = bf16[32,4224]{1,0:T(8,128)(2,1)} fusion(bf16[32,16]{1,0:T(8,128)(2,1)S(1)} %copy.35, bf16[32,2048]{1,0:T(8,128)(2,1)} %param.9, bf16[32,2048]{1,0:T(8,128)(2,1)} %param.8), kind=kLoop, calls=%fused_computation.33 | loop fusion | flops 1081344 | bytes 533504 | tf_op jit(solution)/shard_map/concatenate | solution.py:513
  5.5 47.5 %shard_map.111 = bf16[32,32,4224]{2,1,0:T(8,128)(2,1)} custom-call(bf16[32,4224]{1,0:T(8,128)(2,1)} %fusion.23.source), custom_call_target="tpu_custom_call" | custom-call | tf_op jit(solution)/shard_map/pallas_call | solution.py:386
  53.0 1.0 slice.29
  54.0 0.8 constant_dynamic-slice_fusion
  54.8 1.1 %copy.45 = bf16[1024,2]{0,1:T(2,128)(2,1)S(1)} copy(bf16[1024,2]{1,0:T(8,128)(2,1)} %constant_dynamic-slice_fusion) | data formatting | bytes 8192
  56.0 0.0 copy-done
  56.0 0.0 slice-start.1
  56.0 0.0 slice-start.2
  56.0 0.0 copy-start.2
  56.0 5.4 %fusion.9 = f32[2,1024,2,192]{1,3,2,0:T(8,128)S(1)} fusion(bf16[2,2,192,2048]{3,2,1,0:T(8,128)(2,1)S(1)} %copy-done, bf16[1024,4224]{1,0:T(8,128)(2,1)} %bitcast.58), kind=kOutput, calls=%fused_computation.15 | convolution fusion | flops 3221225472 | bytes 10485760 | tf_op jit(solution)/shard_map/td,ejfd->jtef/dot_general | solution.py:521
  61.4 0.0 slice-done
  61.5 2.7 %fusion.21 = (bf16[1,1024,2,192]{1,3,2,0:T(8,128)(2,1)S(1)}, bf16[1,1024,2,192]{1,3,2,0:T(8,128)(2,1)S(1)}, f32[1024,2]{0,1:T(2,128)S(1)}, bf16[1024,2,192]{0,2,1:T(8,128)(2,1)S(1)}) fusion(f32[2,1024,2,192]{1,3,2,0:T(8,128)S(1)} %fusion.9, f32[1024,2]{0,1:T(2,128)S(1)} %convert_element_type.41, bf16[2,192,2048]{2,1,0:T(8,128)(2,1)S(1)} %copy-done.2, ...), kind=kOutput, calls=%fused_computation.30 | convolution fusion | flops 1618081792 | bytes 11288576 | tf_op jit(solution)/shard_map/td,efd->tef/dot_general | solution.py:522
  64.2 0.3 select_reduce_fusion
  64.5 3.0 %fusion.8 = bf16[2,192,2048]{2,1,0:T(8,128)(2,1)} fusion(bf16[1024,4224]{1,0:T(8,128)(2,1)S(1)} %bitcast.62, bf16[1024,2,192]{0,2,1:T(8,128)(2,1)S(1)} %get-tuple-element.25, f32[1024,2]{0,1:T(2,128)S(1)} %convert_element_type.41), kind=kOutput, calls=%fused_computation.12 | convolution fusion | flops 1612578816 | bytes 6561792 | tf_op jit(solution)/shard_map/tef,td->efd/dot_general | solution.py:546
  67.5 0.1 pad_maximum_fusion.1
  67.6 3.4 %fusion.2 = f32[2048,768]{0,1:S(1)} fusion(bf16[1024,768]{0,1:T(8,128)(2,1)S(1)} %bitcast.65, bf16[1024,4224]{1,0:T(8,128)(2,1)S(1)} %bitcast.63), kind=kOutput, calls=%fused_computation.5 | convolution fusion | flops 3221225472 | bytes 12058624
  71.1 0.5 convert_bitcast_fusion
  71.5 2.0 %copy.40 = bf16[2,2,192,2048]{3,2,1,0:T(8,128)(2,1)} copy(bf16[2,2,192,2048]{3,2,0,1:T(8,128)(2,1)S(1)} %convert_bitcast_fusion) | data formatting | bytes 6291456
  73.6 3.7 %bitcast_convert_fusion = bf16[1024,2048]{1,0:T(8,128)(2,1)S(1)} fusion(bf16[2,2,192,2048]{3,2,1,0:T(8,128)(2,1)S(1)} %copy-done, bf16[1,1024,2,192]{1,3,2,0:T(8,128)(2,1)S(1)} %get-tuple-element.23, bf16[1,1024,2,192]{1,3,2,0:T(8,128)(2,1)S(1)} %get-tuple-element.22), kind=kOutput, calls=%fused_computation | convolution fusion | flops 3224109056 | bytes 8912896 | tf_op jit(solution)/shard_map/jtef,ejfd->td/dot_general | solution.py:533
  77.3 0.4 pad_maximum_fusion
  77.7 0.0 copy-start.1
  77.7 30.8 %shard_map.112 = bf16[32,2176]{1,0:T(8,128)(2,1)S(1)} custom-call(bf16[4,4,2,32,2176]{4,3,2,1,0:T(8,128)(2,1)S(1)} %bitcast.56), custom_call_target="tpu_custom_call" | custom-call | tf_op jit(solution)/shard_map/pallas_call | solution.py:481
  108.6 0.7 slice.26
  109.3 0.1 copy.39
  109.3 0.6 select_reduce_fusion.1
  (9 shorter events, 0.0 us)
Async XLA Ops:
  0.6 55.3 %copy-start = (bf16[2,2,192,2048]{3,2,1,0:T(8,128)(2,1)S(1)}, bf16[2,2,192,2048]{3,2,1,0:T(8,128)(2,1)}, u32[]{:S(2)}) copy-start(bf16[2,2,192,2048]{3,2,1,0:T(8,128)(2,1)} %param.14) | copy-start | bytes 9437188
  54.8 6.6 %slice-start = ((s8[8650752]{0:T(1024)(128)(4,1)}), s8[262144]{0:T(1024)(128)(4,1)S(1)}, s32[]{:S(2)}) async-start(s8[8650752]{0:T(1024)(128)(4,1)} %bitcast.59), calls=%async_computation | async-start | bytes 524288
  56.0 5.5 %slice-start.1 = ((s8[8650752]{0:T(1024)(128)(4,1)}), s8[4194304]{0:T(1024)(128)(4,1)S(1)}, s32[]{:S(2)}) async-start(s8[8650752]{0:T(1024)(128)(4,1)} %bitcast.59), calls=%async_computation.1 | async-start | bytes 8388608
  56.0 5.5 %slice-start.2 = ((s8[8650752]{0:T(1024)(128)(4,1)}), s8[4194304]{0:T(1024)(128)(4,1)S(1)}, s32[]{:S(2)}) async-start(s8[8650752]{0:T(1024)(128)(4,1)} %bitcast.59), calls=%async_computation.2 | async-start | bytes 8388608
  56.0 5.5 %copy-start.2 = (bf16[2,192,2048]{2,1,0:T(8,128)(2,1)S(1)}, bf16[2,192,2048]{2,1,0:T(8,128)(2,1)}, u32[]{:S(2)}) copy-start(bf16[2,192,2048]{2,1,0:T(8,128)(2,1)} %param.15) | copy-start | bytes 4718596
  77.7 31.6 %copy-start.1 = (s32[32,8]{0,1:T(8,128)S(1)}, s32[32,8]{0,1:T(8,128)}, u32[]{:S(2)}) copy-start(s32[32,8]{0,1:T(8,128)} %param.10) | copy-start | bytes 3076

commit v3 on v0

--- a/solution.py
+++ b/solution.py
@@ -1,7 +1,13 @@
+import functools
+
 import jax
 import jax.numpy as jnp
 from jax import lax
+from jax.experimental import pallas as pl
+from jax.experimental.pallas import tpu as pltpu
 from jax.sharding import PartitionSpec as P
+
+MESH = pl.DeviceIdType.MESH
 
 
 def lookup(values_table, indices):
@@ -218,6 +224,427 @@
     return (grad_tokens, grad_gates, jnp.stack(grad_gu, axis=0), jnp.stack(grad_down, axis=0))
 
 
+def chosen_gates(routing, replica, gates, host_expert, experts):
+    listed = jnp.any(routing[:, :, None] == host_expert[None, None, :], axis=2)
+    usable = (replica == 0) | listed
+    picks = usable[:, :, None] & (
+        routing[:, :, None] == lax.broadcasted_iota(jnp.int32, routing.shape + (experts,), 2)
+    )
+    weights = jnp.sum(jnp.where(picks, gates.astype(jnp.float32)[:, :, None], 0.0), axis=1)
+    return (picks, weights)
+
+
+def greet(partners):
+    barrier = pltpu.get_barrier_semaphore()
+    for condition, device in partners:
+
+        @pl.when(condition)
+        def _():
+            pl.semaphore_signal(barrier, inc=1, device_id=device, device_id_type=MESH)
+
+    pl.semaphore_wait(barrier, sum(condition.astype(jnp.int32) for condition, _ in partners))
+
+
+def fused_kernel(
+    depth,
+    features,
+    source,
+    gu_hbm,
+    down_hbm,
+    summed_ref,
+    grad_gu_hbm,
+    grad_down_hbm,
+    rows_ref,
+    gu_ref,
+    down_ref,
+    grad_gu_ref,
+    grad_down_ref,
+    mixed_ref,
+    hidden_ref,
+    part_ref,
+    paired,
+    ready,
+    crossed,
+    column_ref,
+    risen,
+    total,
+    sent,
+    landed,
+    local,
+    sums_sent,
+    sums_landed,
+):
+    dp = lax.axis_index("dp")
+    expert = lax.axis_index("expert")
+    height, core = expert // 2, expert % 2
+    row, column = dp // 2, dp % 2
+    across = row * 2 + 1 - column
+    along = (1 - row) * 2 + column
+    diagonal = (1 - row) * 2 + 1 - column
+    roles = (dp, across, along, diagonal)
+    count, half = source.shape[0], source.shape[0] // 2
+    owned = down_ref.shape[0]
+    group_slots = 2 * depth
+    group_rows = group_slots * count
+    lanes = source.shape[1] - 2 * features
+    partner = (dp, height * 2 + 1 - core)
+    x_device = (across, expert)
+    y_device = (along, expert)
+    up_device = (dp, jnp.minimum(expert + 2, 2 * depth - 1))
+    down_device = (dp, jnp.maximum(expert - 2, 0))
+    has_up = height < depth - 1
+    has_down = height > 0
+    always = height >= 0
+    levels = [lax.rem(height + step, depth) for step in range(1, depth)] + [height]
+    loads = [
+        pltpu.make_async_copy(gu_hbm, gu_ref, local.at[1]),
+        pltpu.make_async_copy(down_hbm, down_ref, local.at[2]),
+    ]
+    for load in loads:
+        load.start()
+    greet(
+        [
+            (always, partner),
+            (always, x_device),
+            (always, y_device),
+            (always, (diagonal, expert)),
+        ]
+        + [(always, (dp, level * 2 + core)) for level in levels[:-1]]
+    )
+
+    def slot_of(dp_from, height_from, core_from):
+        return (dp_from * depth + height_from) * 2 + core_from
+
+    def copy(slot, way, device, part=None, own=False):
+        block = source if own else rows_ref.at[slot]
+        into = rows_ref.at[slot]
+        piece = 0
+        if part is not None:
+            block = block.at[pl.ds(part * half, half)]
+            into = into.at[pl.ds(part * half, half)]
+            piece = part
+        return pltpu.make_async_remote_copy(
+            src_ref=block,
+            dst_ref=into,
+            send_sem=sent.at[slot, way * 2 + piece],
+            recv_sem=landed.at[slot, piece],
+            device_id=device,
+            device_id_type=MESH,
+        )
+
+    finish = []
+
+    def guard(condition, action):
+        if condition is always:
+            action()
+        else:
+            pl.when(condition)(action)
+
+    def send(condition, *args, **kwargs):
+        finish.append((condition, args, kwargs))
+        guard(condition, lambda: copy(*args, **kwargs).start())
+
+    def arrive(condition, slot, part=None):
+        guard(condition, lambda: copy(slot, 0, partner, part).wait_recv())
+
+    def both(first, second):
+        return first if second is always else jnp.logical_and(first, second)
+
+    steps = [[(always, height)]]
+    for distance in range(1, depth):
+        steps.append([(height >= distance, jnp.maximum(height - distance, 0))])
+        steps[-1].append(
+            (height + distance < depth, jnp.minimum(height + distance, depth - 1))
+        )
+
+    def relay_column(index):
+        for side, (condition, level) in enumerate(steps[index]):
+            slot = slot_of(dp, level, core)
+            arrive(condition, slot)
+            if side == 0:
+                send(both(condition, has_up), slot, 3, up_device)
+            else:
+                send(both(condition, has_down), slot, 4, down_device)
+            send(condition, slot, 1, x_device)
+            send(condition, slot, 2, y_device)
+            send(condition, slot, 0, partner)
+
+    def relay_sides(index):
+        for condition, level in steps[index]:
+            slot = slot_of(across, level, core)
+            arrive(condition, slot)
+            send(condition, slot, 2, y_device, part=0)
+            send(condition, slot, 0, partner)
+            slot = slot_of(along, level, core)
+            arrive(condition, slot)
+            send(condition, slot, 1, x_device, part=1)
+            send(condition, slot, 0, partner)
+
+    def relay_diagonal(index):
+        for condition, level in steps[index]:
+            slot = slot_of(diagonal, level, core)
+            for part in range(2):
+                arrive(condition, slot, part)
+                send(condition, slot, 0, partner, part=part)
+
+    def partner_rows(role):
+        for level in range(depth):
+            slot = slot_of(roles[role], level, 1 - core)
+            if role == 3:
+                arrive(always, slot, 0)
+                arrive(always, slot, 1)
+            else:
+                arrive(always, slot)
+
+    def remote(block, into, index, device):
+        return pltpu.make_async_remote_copy(
+            src_ref=block,
+            dst_ref=into,
+            send_sem=sums_sent.at[index],
+            recv_sem=sums_landed.at[index],
+            device_id=device,
+            device_id_type=MESH,
+        )
+
+    def pair_copy(role):
+        return remote(part_ref.at[roles[role], :, 1 - core], paired.at[role], role, partner)
+
+    def cross_copy(step, way):
+        return remote(
+            ready.at[step, way],
+            crossed.at[step, way],
+            4 + step * 3 + way,
+            (roles[way + 1], expert),
+        )
+
+    def rise_copy(step):
+        return remote(
+            column_ref.at[step],
+            risen.at[step],
+            4 + 3 * depth + step,
+            (dp, levels[step] * 2 + core),
+        )
+
+    def group(role):
+        return pl.ds(roles[role] * group_slots, group_slots)
+
+    def rows_by_columns(a, b):
+        return lax.dot_general(
+            a, b, (((1,), (1,)), ((), ())), preferred_element_type=jnp.float32
+        )
+
+    def compute(role):
+        inputs = rows_ref[group(role), :, :features].reshape(group_rows, features)
+        upstream = rows_ref[group(role), :, features : 2 * features].reshape(
+            group_rows, features
+        )
+        side = rows_ref[group(role), :, 2 * features :].reshape(group_rows, lanes)
+        side = side.astype(jnp.float32)
+        slots = lax.broadcasted_iota(jnp.int32, side.shape, 1)
+        gate_side = jnp.zeros(side.shape, jnp.float32)
+        for local_expert in range(owned):
+            at_expert = slots == expert * owned + local_expert
+            weight = jnp.sum(jnp.where(at_expert, side, 0.0), axis=1, keepdims=True)
+            gate_pre = rows_by_columns(inputs, gu_ref[local_expert, 0])
+            up_part = rows_by_columns(inputs, gu_ref[local_expert, 1])
+            raw_hidden = rows_by_columns(upstream, down_ref[local_expert])
+            sigmoid_gate = jax.nn.sigmoid(gate_pre)
+            active = gate_pre * sigmoid_gate
+            hidden = (active * up_part).astype(jnp.bfloat16).astype(jnp.float32)
+            gate_part = jnp.sum(hidden * raw_hidden, axis=1, keepdims=True)
+            gate_side = jnp.where(at_expert, gate_part, gate_side)
+            grad_hidden = raw_hidden * weight
+            grad_gate = (
+                grad_hidden * up_part * sigmoid_gate * (1.0 + gate_pre * (1.0 - sigmoid_gate))
+            )
+            hidden_ref[local_expert, roles[role]] = (hidden * weight).astype(jnp.bfloat16)
+            mixed_ref[2 * local_expert, roles[role]] = grad_gate.astype(jnp.bfloat16)
+            mixed_ref[2 * local_expert + 1, roles[role]] = (grad_hidden * active).astype(
+                jnp.bfloat16
+            )
+        dx = jnp.zeros((group_rows, features), jnp.float32)
+        for index in range(2 * owned):
+            dx = dx + jnp.dot(
+                mixed_ref[index, roles[role]],
+                gu_ref[index // 2, index % 2],
+                preferred_element_type=jnp.float32,
+            )
+        shape = (depth, 2, count)
+        part_ref[roles[role], :, :, :, :features] = dx.astype(jnp.bfloat16).reshape(
+            shape + (features,)
+        )
+        part_ref[roles[role], :, :, :, features:] = gate_side.astype(jnp.bfloat16).reshape(
+            shape + (lanes,)
+        )
+        pair_copy(role).start()
+
+    def combine(role):
+        pair_copy(role).wait_recv()
+        if role > 0:
+            for step in range(depth):
+                ready[step, role - 1] = (
+                    part_ref[roles[role], levels[step], core].astype(jnp.float32)
+                    + paired[role, levels[step]].astype(jnp.float32)
+                ).astype(jnp.bfloat16)
+                cross_copy(step, role - 1).start()
+
+    def columns_by_columns(a, b):
+        return lax.dot_general(
+            a, b, (((0,), (0,)), ((), ())), preferred_element_type=jnp.float32
+        ).astype(jnp.bfloat16)
+
+    total_rows = 4 * group_rows
+    quarter = mixed_ref.shape[3]
+
+    def down_grads():
+        upstream = rows_ref[:, :, features : 2 * features].reshape(total_rows, features)
+        for local_expert in range(owned):
+            weighted = hidden_ref[local_expert].reshape(total_rows, quarter)
+            grad_down_ref[local_expert] = columns_by_columns(weighted, upstream)
+        pltpu.make_async_copy(grad_down_ref, grad_down_hbm, local.at[2]).start()
+
+    def gu_grads():
+        inputs = rows_ref[:, :, :features].reshape(total_rows, features)
+        for index in range(2 * owned):
+            grads = mixed_ref[index].reshape(total_rows, quarter)
+            grad_gu_ref[index // 2, index % 2] = columns_by_columns(grads, inputs)
+        pltpu.make_async_copy(grad_gu_ref, grad_gu_hbm, local.at[1]).start()
+
+    mine = slot_of(dp, height, core)
+    send(has_up, mine, 3, up_device, own=True)
+    send(has_down, mine, 4, down_device, own=True)
+    send(always, mine, 1, x_device, own=True)
+    send(always, mine, 2, y_device, own=True)
+    send(always, mine, 0, partner, own=True)
+    keep = pltpu.make_async_copy(source, rows_ref.at[mine], local.at[0])
+    keep.start()
+    for index in range(1, depth):
+        relay_column(index)
+        relay_sides(index - 1)
+    keep.wait()
+    for load in loads:
+        load.wait()
+    partner_rows(0)
+    compute(0)
+    relay_sides(depth - 1)
+    relay_diagonal(0)
+    partner_rows(1)
+    compute(1)
+    for index in range(1, depth - 1):
+        relay_diagonal(index)
+    partner_rows(2)
+    compute(2)
+    combine(0)
+    combine(1)
+    relay_diagonal(depth - 1)
+    partner_rows(3)
+    compute(3)
+    combine(2)
+    down_grads()
+    combine(3)
+    gu_grads()
+    for step in range(depth):
+        for way in range(3):
+            cross_copy(step, way).wait_recv()
+        summed = part_ref[dp, levels[step], core].astype(jnp.float32) + paired[
+            0, levels[step]
+        ].astype(jnp.float32)
+        for way in range(3):
+            summed = summed + crossed[step, way].astype(jnp.float32)
+        if step < depth - 1:
+            column_ref[step] = summed.astype(jnp.bfloat16)
+            rise_copy(step).start()
+        else:
+            total[...] = summed
+    for step in range(depth - 1):
+        rise_copy(step).wait_recv()
+        total[...] = total[...] + risen[step].astype(jnp.float32)
+    summed_ref[...] = total[...].astype(jnp.bfloat16)
+    for condition, args, kwargs in finish:
+        guard(condition, lambda args=args, kwargs=kwargs: copy(*args, **kwargs).wait_send())
+    for role in range(4):
+        pair_copy(role).wait_send()
+    for step in range(depth):
+        for way in range(3):
+            cross_copy(step, way).wait_send()
+        if step < depth - 1:
+            rise_copy(step).wait_send()
+    pltpu.make_async_copy(grad_down_ref, grad_down_hbm, local.at[2]).wait()
+    pltpu.make_async_copy(grad_gu_ref, grad_gu_hbm, local.at[1]).wait()
+
+
+def fused_layer(payload, w_gate_up, w_down, expert_size):
+    count, width = payload.shape
+    features = w_down.shape[2]
+    owned, quarter = w_down.shape[:2]
+    depth = expert_size // 2
+    slots = 4 * expert_size
+    sums = width - features
+    block = (count, sums)
+    group_rows = expert_size * count
+    kind = jnp.bfloat16
+    anywhere = pl.BlockSpec(memory_space=pl.ANY)
+    return pl.pallas_call(
+        functools.partial(fused_kernel, depth, features),
+        out_shape=(
+            jax.ShapeDtypeStruct(block, kind),
+            jax.ShapeDtypeStruct(w_gate_up.shape, kind),
+            jax.ShapeDtypeStruct(w_down.shape, kind),
+        ),
+        in_specs=[anywhere] * 3,
+        out_specs=(pl.BlockSpec(memory_space=pltpu.VMEM), anywhere, anywhere),
+        scratch_shapes=[
+            pltpu.VMEM((slots, count, width), kind),
+            pltpu.VMEM(w_gate_up.shape, kind),
+            pltpu.VMEM(w_down.shape, kind),
+            pltpu.VMEM(w_gate_up.shape, kind),
+            pltpu.VMEM(w_down.shape, kind),
+            pltpu.VMEM((2 * owned, 4, group_rows, quarter), kind),
+            pltpu.VMEM((owned, 4, group_rows, quarter), kind),
+            pltpu.VMEM((4, depth, 2) + block, kind),
+            pltpu.VMEM((4, depth) + block, kind),
+            pltpu.VMEM((depth, 3) + block, kind),
+            pltpu.VMEM((depth, 3) + block, kind),
+            pltpu.VMEM((depth,) + block, kind),
+            pltpu.VMEM((depth,) + block, kind),
+            pltpu.VMEM(block, jnp.float32),
+            pltpu.SemaphoreType.DMA((slots, 10)),
+            pltpu.SemaphoreType.DMA((slots, 2)),
+            pltpu.SemaphoreType.DMA((3,)),
+            pltpu.SemaphoreType.DMA((4 + 4 * depth,)),
+            pltpu.SemaphoreType.DMA((4 + 4 * depth,)),
+        ],
+        compiler_params=pltpu.CompilerParams(
+            collective_id=0, has_side_effects=True, vmem_limit_bytes=60 << 20
+        ),
+    )(payload, w_gate_up, w_down)
+
+
+def gathered_shards(
+    tokens, grad_out, routing, replica, gates, host_expert, w_gate_up, w_down
+):
+    devices = lax.axis_size("expert")
+    features = tokens.shape[1]
+    owned = w_gate_up.shape[0]
+    experts = owned * devices
+    lanes = (experts + 127) // 128 * 128
+    picks, weights = chosen_gates(routing, replica, gates, host_expert, experts)
+    side = jnp.pad(weights.astype(jnp.bfloat16), ((0, 0), (0, lanes - experts)))
+    payload = jnp.concatenate([tokens, grad_out, side], axis=1)
+    summed, grad_gu, grad_down = fused_layer(payload, w_gate_up, w_down, devices)
+    grad_tokens = summed[:, :features]
+    sums = summed[:, features : features + experts].astype(jnp.float32)
+    grad_gates = jnp.sum(jnp.where(picks, sums[:, None, :], 0.0), axis=2)
+    return (grad_tokens, grad_gates, grad_gu, grad_down)
+
+
+def serve(tokens, grad_out, routing, replica, gates, host_expert, w_gate_up, w_down):
+    squares = lax.axis_size("dp") == 4 and lax.axis_size("expert") % 2 == 0
+    visits_all = routing.shape[1] >= lax.axis_size("expert")
+    body = gathered_shards if squares and visits_all else shards
+    return body(tokens, grad_out, routing, replica, gates, host_expert, w_gate_up, w_down)
+
+
 def solution(mesh):
     in_specs = (
         P(("dp", "expert"), None),
@@ -235,4 +662,4 @@
         P("expert", None, "dp", None),
         P("expert", "dp", None),
     )
-    return jax.shard_map(shards, mesh=mesh, in_specs=in_specs, out_specs=out_specs, check_vma=False)
+    return jax.shard_map(serve, mesh=mesh, in_specs=in_specs, out_specs=out_specs, check_vma=False)

time: 548 us -> 95.6 us (0.17)
  waiting for transfers between devices: 272 us -> 0 us
  blocking collectives: 123 us -> 0 us
  Pallas kernels: 0 us -> 81.7 us
  starting transfers between devices: 39.4 us -> 0 us
  matrix products: 36.4 us -> 0 us
  local copies, waits for them, and re-layouts: 35.9 us -> 6.97 us
  between operations: 17.8 us -> 0.66 us
  other arithmetic: 21.5 us -> 5.95 us
    all_to_all x10 -> x0, waiting for transfers between devices: 249 us -> none  [the longest x1 36.7 us: shards(): lax.all_to_all(source_gu.reshape(2, devices, piece_rows, features), 'expe...]
    all_to_all x3 -> x0, blocking collectives: 115 us -> none  [the longest x1 55.2 us: shards(): lax.all_to_all(row_x.reshape(blocks, lane_rows, features), 'expert', spli...]
    pallas_call x0 -> x1, Pallas kernels: none -> 81.7 us  [fused_layer(): pl.pallas_call(functools.partial(fused_kernel, depth, features), out_shap...]
    all_to_all x10 -> x0, starting transfers between devices: 39.1 us -> none  [the longest x1 4.59 us: shards(): lax.all_to_all(row_dg, 'expert', split_axis=1, concat_axis=1, tiled=True)]
    dot_general x21 -> x0, matrix products: 36.4 us -> none  [the longest x3 8.42 us: expert_block(): jnp.einsum('rd,jfd->jrf', inputs, gate_up, preferred_element_type=jnp.flo...]
    unnamed x5 -> x0, waiting for transfers between devices: 23.3 us -> none
    all_gather x1 -> x0, blocking collectives: 8.25 us -> none  [shards(): lax.all_gather(sent_gate, 'dp', axis=1, tiled=True)]
    all_to_all x9 -> x0, local copies, waits for them, and re-layouts: 7.77 us -> none  [the longest x1 2.29 us: shards(): lax.all_to_all(row_dy.reshape(blocks, lane_rows, features), 'expert', spl...]
  transfers between devices with their start and end apart: 14 -> 0, of which waited for: 11 -> 0; matrix products, arithmetic and copies ran while one was open for 8% -> 0% of each run, Pallas kernels for 0% -> 0%
where the time goes in v3:
time: 95.6 us; the launch traced here: 95.3 us
  Pallas kernels  81.7 us (85%)
  local copies, waits for them, and re-layouts  6.97 us (7%)
  other arithmetic  5.95 us (6%)
    pallas_call x1, Pallas kernels, fused_layer(): pl.pallas_call(functools.partial(fused_kernel, depth, features), out_shap...  81.7 us
    unnamed x6, local copies, waits for them, and re-layouts  5.24 us

profile of v3, /device:TPU:0, one launch (start us, length us, event | category | flops | bytes accessed | tf_op | source)
XLA Modules:
  0.0 95.3 jit_solution(8590913730055413207)
XLA Ops:
  0.6 0.0 copy-start.1
  0.6 0.8 compare_reduce_fusion
  1.5 0.7 compare_or_fusion
  2.2 0.7 convert_element_type.11
  2.9 0.7 select_reduce_fusion.1
  3.6 0.1 copy.18
  3.7 1.7 %fusion.1.source = bf16[32,4224]{1,0:T(8,128)(2,1)} fusion(bf16[32,16]{1,0:T(8,128)(2,1)S(1)} %copy.18, bf16[32,2048]{1,0:T(8,128)(2,1)} %param.9, bf16[32,2048]{1,0:T(8,128)(2,1)} %param.8), kind=kLoop, calls=%fused_computation.2 | loop fusion | flops 1081344 | bytes 533504 | tf_op jit(solution)/shard_map/concatenate | solution.py:633
  5.4 81.7 %shard_map.111 = (bf16[32,2176]{1,0:T(8,128)(2,1)}, bf16[2,2,192,2048]{3,2,1,0:T(8,128)(2,1)}, bf16[2,192,2048]{2,1,0:T(8,128)(2,1)}) custom-call(bf16[32,4224]{1,0:T(8,128)(2,1)} %fusion.1.source, bf16[2,2,192,2048]{3,2,1,0:T(8,128)(2,1)} %gu_hbm.1, bf16[2,192,2048]{2,1,0:T(8,128)(2,1)} %down_hbm.1), custom_call_target="tpu_custom_call" | custom-call | tf_op jit(solution)/shard_map/pallas_call | solution.py:587
  87.1 0.7 slice_convert_fusion
  87.8 0.1 copy.19
  87.9 0.0 copy-done.1
  87.9 0.6 select_reduce_fusion
  88.5 1.6 %slice.6 = bf16[32,2048]{1,0:T(8,128)(2,1)} slice(bf16[32,2176]{1,0:T(8,128)(2,1)} %get-tuple-element.7), slice={[0:32], [0:2048]} | slice | bytes 262144 | tf_op jit(solution)/shard_map/slice | solution.py:635
  90.1 0.0 copy-start
  90.1 4.1 %copy.22 = bf16[2,2,192,2048]{3,2,1,0:T(8,128)(2,1)} copy(bf16[2,2,192,2048]{3,2,1,0:T(8,128)(2,1)} %get-tuple-element.16) | data formatting | bytes 6291456
  94.2 0.0 copy-done
  94.2 1.1 %copy.23 = bf16[2,192,2048]{2,1,0:T(8,128)(2,1)} copy(bf16[2,192,2048]{2,1,0:T(8,128)(2,1)S(1)} %copy-done) | data formatting | bytes 3145728
Async XLA Ops:
  0.6 87.3 %copy-start.1 = (s32[32,8]{0,1:T(8,128)S(1)}, s32[32,8]{0,1:T(8,128)}, u32[]{:S(2)}) copy-start(s32[32,8]{0,1:T(8,128)} %param.10) | copy-start | bytes 3076
  90.1 4.1 %copy-start = (bf16[2,192,2048]{2,1,0:T(8,128)(2,1)S(1)}, bf16[2,192,2048]{2,1,0:T(8,128)(2,1)}, u32[]{:S(2)}) copy-start(bf16[2,192,2048]{2,1,0:T(8,128)(2,1)} %get-tuple-element.17) | copy-start | bytes 4718596

commit v4 on v3

--- a/solution.py
+++ b/solution.py
@@ -248,7 +248,9 @@
 def fused_kernel(
     depth,
     features,
-    source,
+    tokens_hbm,
+    upstream_hbm,
+    side_hbm,
     gu_hbm,
     down_hbm,
     summed_ref,
@@ -282,11 +284,11 @@
     along = (1 - row) * 2 + column
     diagonal = (1 - row) * 2 + 1 - column
     roles = (dp, across, along, diagonal)
-    count, half = source.shape[0], source.shape[0] // 2
+    count, half = tokens_hbm.shape[0], tokens_hbm.shape[0] // 2
     owned = down_ref.shape[0]
     group_slots = 2 * depth
     group_rows = group_slots * count
-    lanes = source.shape[1] - 2 * features
+    lanes = side_hbm.shape[1]
     partner = (dp, height * 2 + 1 - core)
     x_device = (across, expert)
     y_device = (along, expert)
@@ -300,7 +302,17 @@
         pltpu.make_async_copy(gu_hbm, gu_ref, local.at[1]),
         pltpu.make_async_copy(down_hbm, down_ref, local.at[2]),
     ]
-    for load in loads:
+    mine = (dp * depth + height) * 2 + core
+    keeps = [
+        pltpu.make_async_copy(tokens_hbm, rows_ref.at[mine, :, pl.ds(0, features)], local.at[0]),
+        pltpu.make_async_copy(
+            upstream_hbm, rows_ref.at[mine, :, pl.ds(features, features)], local.at[3]
+        ),
+        pltpu.make_async_copy(
+            side_hbm, rows_ref.at[mine, :, pl.ds(2 * features, lanes)], local.at[4]
+        ),
+    ]
+    for load in keeps + loads:
         load.start()
     greet(
         [
@@ -315,8 +327,8 @@
     def slot_of(dp_from, height_from, core_from):
         return (dp_from * depth + height_from) * 2 + core_from
 
-    def copy(slot, way, device, part=None, own=False):
-        block = source if own else rows_ref.at[slot]
+    def copy(slot, way, device, part=None):
+        block = rows_ref.at[slot]
         into = rows_ref.at[slot]
         piece = 0
         if part is not None:
@@ -387,9 +399,13 @@
                 arrive(condition, slot, part)
                 send(condition, slot, 0, partner, part=part)
 
-    def partner_rows(role):
-        for level in range(depth):
-            slot = slot_of(roles[role], level, 1 - core)
+    span = depth // 2
+    near = height // span * span
+    far = span - near
+
+    def partner_rows(role, start=0, size=depth):
+        for level in range(size):
+            slot = slot_of(roles[role], start + level, 1 - core)
             if role == 3:
                 arrive(always, slot, 0)
                 arrive(always, slot, 1)
@@ -406,8 +422,13 @@
             device_id_type=MESH,
         )
 
-    def pair_copy(role):
-        return remote(part_ref.at[roles[role], :, 1 - core], paired.at[role], role, partner)
+    def pair_copy(role, start=0, size=depth):
+        return remote(
+            part_ref.at[roles[role], pl.ds(start, size), 1 - core],
+            paired.at[role, pl.ds(start, size)],
+            role if size == depth else 4 + 4 * depth + start // span,
+            partner,
+        )
 
     def cross_copy(step, way):
         return remote(
@@ -425,20 +446,22 @@
             (dp, levels[step] * 2 + core),
         )
 
-    def group(role):
-        return pl.ds(roles[role] * group_slots, group_slots)
+    def group(role, start, size):
+        return pl.ds(roles[role] * group_slots + 2 * start, 2 * size)
 
     def rows_by_columns(a, b):
         return lax.dot_general(
             a, b, (((1,), (1,)), ((), ())), preferred_element_type=jnp.float32
         )
 
-    def compute(role):
-        inputs = rows_ref[group(role), :, :features].reshape(group_rows, features)
-        upstream = rows_ref[group(role), :, features : 2 * features].reshape(
-            group_rows, features
-        )
-        side = rows_ref[group(role), :, 2 * features :].reshape(group_rows, lanes)
+    def compute(role, start=0, size=depth):
+        tall = size * 2 * count
+        span_rows = pl.ds(pl.multiple_of(start * 2 * count, 2 * count), tall)
+        inputs = rows_ref[group(role, start, size), :, :features].reshape(tall, features)
+        upstream = rows_ref[group(role, start, size), :, features : 2 * features].reshape(
+            tall, features
+        )
+        side = rows_ref[group(role, start, size), :, 2 * features :].reshape(tall, lanes)
         side = side.astype(jnp.float32)
         slots = lax.broadcasted_iota(jnp.int32, side.shape, 1)
         gate_side = jnp.zeros(side.shape, jnp.float32)
@@ -457,36 +480,45 @@
             grad_gate = (
                 grad_hidden * up_part * sigmoid_gate * (1.0 + gate_pre * (1.0 - sigmoid_gate))
             )
-            hidden_ref[local_expert, roles[role]] = (hidden * weight).astype(jnp.bfloat16)
-            mixed_ref[2 * local_expert, roles[role]] = grad_gate.astype(jnp.bfloat16)
-            mixed_ref[2 * local_expert + 1, roles[role]] = (grad_hidden * active).astype(
+            hidden_ref[local_expert, roles[role], span_rows] = (hidden * weight).astype(jnp.bfloat16)
+            mixed_ref[2 * local_expert, roles[role], span_rows] = grad_gate.astype(jnp.bfloat16)
+            mixed_ref[2 * local_expert + 1, roles[role], span_rows] = (grad_hidden * active).astype(
                 jnp.bfloat16
             )
-        dx = jnp.zeros((group_rows, features), jnp.float32)
+        dx = jnp.zeros((tall, features), jnp.float32)
         for index in range(2 * owned):
             dx = dx + jnp.dot(
-                mixed_ref[index, roles[role]],
+                mixed_ref[index, roles[role], span_rows],
                 gu_ref[index // 2, index % 2],
                 preferred_element_type=jnp.float32,
             )
-        shape = (depth, 2, count)
-        part_ref[roles[role], :, :, :, :features] = dx.astype(jnp.bfloat16).reshape(
+        shape = (size, 2, count)
+        part_ref[roles[role], pl.ds(start, size), :, :, :features] = dx.astype(jnp.bfloat16).reshape(
             shape + (features,)
         )
-        part_ref[roles[role], :, :, :, features:] = gate_side.astype(jnp.bfloat16).reshape(
+        part_ref[roles[role], pl.ds(start, size), :, :, features:] = gate_side.astype(jnp.bfloat16).reshape(
             shape + (lanes,)
         )
-        pair_copy(role).start()
-
-    def combine(role):
-        pair_copy(role).wait_recv()
+        pair_copy(role, start, size).start()
+
+    def combine(role, start=0, size=depth):
+        pair_copy(role, start, size).wait_recv()
         if role > 0:
-            for step in range(depth):
+            for offset in range(size):
+                level = levels[offset] if size == depth else start + offset
+                step = offset if size == depth else lax.rem(level - height - 1 + depth, depth)
                 ready[step, role - 1] = (
-                    part_ref[roles[role], levels[step], core].astype(jnp.float32)
-                    + paired[role, levels[step]].astype(jnp.float32)
+                    part_ref[roles[role], level, core].astype(jnp.float32)
+                    + paired[role, level].astype(jnp.float32)
                 ).astype(jnp.bfloat16)
-                cross_copy(step, role - 1).start()
+                pltpu.make_async_remote_copy(
+                    src_ref=ready.at[step, role - 1],
+                    dst_ref=crossed.at[step, role - 1],
+                    send_sem=sums_sent.at[4 + step * 3 + role - 1],
+                    recv_sem=sums_landed.at[4 + step * 3 + role - 1],
+                    device_id=(roles[role], expert),
+                    device_id_type=MESH,
+                ).start()
 
     def columns_by_columns(a, b):
         return lax.dot_general(
@@ -510,18 +542,16 @@
             grad_gu_ref[index // 2, index % 2] = columns_by_columns(grads, inputs)
         pltpu.make_async_copy(grad_gu_ref, grad_gu_hbm, local.at[1]).start()
 
-    mine = slot_of(dp, height, core)
-    send(has_up, mine, 3, up_device, own=True)
-    send(has_down, mine, 4, down_device, own=True)
-    send(always, mine, 1, x_device, own=True)
-    send(always, mine, 2, y_device, own=True)
-    send(always, mine, 0, partner, own=True)
-    keep = pltpu.make_async_copy(source, rows_ref.at[mine], local.at[0])
-    keep.start()
+    for keep in keeps:
+        keep.wait()
+    send(has_up, mine, 3, up_device)
+    send(has_down, mine, 4, down_device)
+    send(always, mine, 1, x_device)
+    send(always, mine, 2, y_device)
+    send(always, mine, 0, partner)
     for index in range(1, depth):
         relay_column(index)
         relay_sides(index - 1)
-    keep.wait()
     for load in loads:
         load.wait()
     partner_rows(0)
@@ -530,18 +560,23 @@
     relay_diagonal(0)
     partner_rows(1)
     compute(1)
-    for index in range(1, depth - 1):
+    for index in range(1, span):
         relay_diagonal(index)
     partner_rows(2)
     compute(2)
     combine(0)
     combine(1)
+    for index in range(span, depth - 1):
+        relay_diagonal(index)
+    partner_rows(3, near, span)
+    compute(3, near, span)
+    combine(2)
     relay_diagonal(depth - 1)
-    partner_rows(3)
-    compute(3)
-    combine(2)
+    combine(3, near, span)
+    partner_rows(3, far, span)
+    compute(3, far, span)
     down_grads()
-    combine(3)
+    combine(3, far, span)
     gu_grads()
     for step in range(depth):
         for way in range(3):
@@ -562,8 +597,10 @@
     summed_ref[...] = total[...].astype(jnp.bfloat16)
     for condition, args, kwargs in finish:
         guard(condition, lambda args=args, kwargs=kwargs: copy(*args, **kwargs).wait_send())
-    for role in range(4):
+    for role in range(3):
         pair_copy(role).wait_send()
+    pair_copy(3, near, span).wait_send()
+    pair_copy(3, far, span).wait_send()
     for step in range(depth):
         for way in range(3):
             cross_copy(step, way).wait_send()
@@ -573,9 +610,9 @@
     pltpu.make_async_copy(grad_gu_ref, grad_gu_hbm, local.at[1]).wait()
 
 
-def fused_layer(payload, w_gate_up, w_down, expert_size):
-    count, width = payload.shape
-    features = w_down.shape[2]
+def fused_layer(tokens, grad_out, side, w_gate_up, w_down, expert_size):
+    count, features = tokens.shape
+    width = 2 * features + side.shape[1]
     owned, quarter = w_down.shape[:2]
     depth = expert_size // 2
     slots = 4 * expert_size
@@ -591,7 +628,7 @@
             jax.ShapeDtypeStruct(w_gate_up.shape, kind),
             jax.ShapeDtypeStruct(w_down.shape, kind),
         ),
-        in_specs=[anywhere] * 3,
+        in_specs=[anywhere] * 5,
         out_specs=(pl.BlockSpec(memory_space=pltpu.VMEM), anywhere, anywhere),
         scratch_shapes=[
             pltpu.VMEM((slots, count, width), kind),
@@ -610,14 +647,14 @@
             pltpu.VMEM(block, jnp.float32),
             pltpu.SemaphoreType.DMA((slots, 10)),
             pltpu.SemaphoreType.DMA((slots, 2)),
-            pltpu.SemaphoreType.DMA((3,)),
-            pltpu.SemaphoreType.DMA((4 + 4 * depth,)),
-            pltpu.SemaphoreType.DMA((4 + 4 * depth,)),
+            pltpu.SemaphoreType.DMA((5,)),
+            pltpu.SemaphoreType.DMA((6 + 4 * depth,)),
+            pltpu.SemaphoreType.DMA((6 + 4 * depth,)),
         ],
         compiler_params=pltpu.CompilerParams(
             collective_id=0, has_side_effects=True, vmem_limit_bytes=60 << 20
         ),
-    )(payload, w_gate_up, w_down)
+    )(tokens, grad_out, side, w_gate_up, w_down)
 
 
 def gathered_shards(
@@ -630,8 +667,9 @@
     lanes = (experts + 127) // 128 * 128
     picks, weights = chosen_gates(routing, replica, gates, host_expert, experts)
     side = jnp.pad(weights.astype(jnp.bfloat16), ((0, 0), (0, lanes - experts)))
-    payload = jnp.concatenate([tokens, grad_out, side], axis=1)
-    summed, grad_gu, grad_down = fused_layer(payload, w_gate_up, w_down, devices)
+    summed, grad_gu, grad_down = fused_layer(
+        tokens, grad_out, side, w_gate_up, w_down, devices
+    )
     grad_tokens = summed[:, :features]
     sums = summed[:, features : features + experts].astype(jnp.float32)
     grad_gates = jnp.sum(jnp.where(picks, sums[:, None, :], 0.0), axis=2)
@@ -639,7 +677,7 @@
 
 
 def serve(tokens, grad_out, routing, replica, gates, host_expert, w_gate_up, w_down):
-    squares = lax.axis_size("dp") == 4 and lax.axis_size("expert") % 2 == 0
+    squares = lax.axis_size("dp") == 4 and lax.axis_size("expert") % 4 == 0
     visits_all = routing.shape[1] >= lax.axis_size("expert")
     body = gathered_shards if squares and visits_all else shards
     return body(tokens, grad_out, routing, replica, gates, host_expert, w_gate_up, w_down)

time: 95.6 us -> 96.8 us (1.013)
  Pallas kernels: 81.7 us -> 84.1 us
  other arithmetic: 5.95 us -> 4.25 us
    pallas_call x1, Pallas kernels: 81.7 us -> 84.1 us  [fused_layer(): pl.pallas_call(functools.partial(fused_kernel, depth, features), out_shap...]
    concatenate x1 -> x0, other arithmetic: 1.7 us -> none  [gathered_shards(): payload = jnp.concatenate([tokens, grad_out, side], axis=1)]
where the time goes in v4:
time: 96.8 us; the launch traced here: 96.5 us
  Pallas kernels  84.1 us (87%)
  local copies, waits for them, and re-layouts  7.57 us (8%)
  other arithmetic  4.25 us (4%)
    pallas_call x1, Pallas kernels, fused_layer(): pl.pallas_call(functools.partial(fused_kernel, depth, features), out_shap...  84.1 us
    unnamed x6, local copies, waits for them, and re-layouts  5.24 us

profile of v4, /device:TPU:0, one launch (start us, length us, event | category | flops | bytes accessed | tf_op | source)
XLA Modules:
  0.0 96.5 jit_solution(12396185120628733678)
XLA Ops:
  0.6 0.0 copy-start.1
  0.6 0.8 compare_reduce_fusion
  1.5 0.7 compare_or_fusion
  2.2 0.7 convert_element_type.11
  2.9 0.7 select_reduce_fusion.1
  3.6 0.1 copy.18
  3.7 0.6 pad.4.side_hbm
  4.3 84.1 %shard_map.111 = (bf16[32,2176]{1,0:T(8,128)(2,1)}, bf16[2,2,192,2048]{3,2,1,0:T(8,128)(2,1)}, bf16[2,192,2048]{2,1,0:T(8,128)(2,1)}) custom-call(bf16[32,2048]{1,0:T(8,128)(2,1)} %tokens_hbm.1, bf16[32,2048]{1,0:T(8,128)(2,1)} %upstream_hbm.1, bf16[32,128]{1,0:T(8,128)(2,1)} %pad.4.side_hbm, bf16[2,2,192,2048]{3,2,1,0:T(8,128)(2,1)} %gu_hbm.1, ...), custom_call_target="tpu_custom_call" | custom-call | tf_op jit(solution)/shard_map/pallas_call | solution.py:624
  88.3 0.7 slice_convert_fusion
  89.0 0.1 copy.19
  89.1 0.0 copy-done.1
  89.1 0.6 select_reduce_fusion
  89.7 1.6 %slice.6 = bf16[32,2048]{1,0:T(8,128)(2,1)} slice(bf16[32,2176]{1,0:T(8,128)(2,1)} %get-tuple-element.7), slice={[0:32], [0:2048]} | slice | bytes 262144 | tf_op jit(solution)/shard_map/slice | solution.py:673
  91.3 0.0 copy-start
  91.3 4.1 %copy.22 = bf16[2,2,192,2048]{3,2,1,0:T(8,128)(2,1)} copy(bf16[2,2,192,2048]{3,2,1,0:T(8,128)(2,1)} %get-tuple-element.16) | data formatting | bytes 6291456
  95.4 0.0 copy-done
  95.4 1.1 %copy.23 = bf16[2,192,2048]{2,1,0:T(8,128)(2,1)} copy(bf16[2,192,2048]{2,1,0:T(8,128)(2,1)S(1)} %copy-done) | data formatting | bytes 3145728
Async XLA Ops:
  0.6 88.5 %copy-start.1 = (s32[32,8]{0,1:T(8,128)S(1)}, s32[32,8]{0,1:T(8,128)}, u32[]{:S(2)}) copy-start(s32[32,8]{0,1:T(8,128)} %param.10) | copy-start | bytes 3076
  91.3 4.1 %copy-start = (bf16[2,192,2048]{2,1,0:T(8,128)(2,1)S(1)}, bf16[2,192,2048]{2,1,0:T(8,128)(2,1)}, u32[]{:S(2)}) copy-start(bf16[2,192,2048]{2,1,0:T(8,128)(2,1)} %get-tuple-element.17) | copy-start | bytes 4718596
